TPU v7x, 256 devices: a whole 4x4x8 slice. The times are simulated.
256 devices in a mesh: section: 8 (over z), tm: 32 (over x, y, core).
Axes of the slice: x: 4, y: 4, z: 8, core: 2. Of those that a mesh axis runs over, the one named last changes fastest.
Arguments:
- acts: bfloat16 [8, 2, 2048, 1024], P('section', None, 'tm'), may hold values from -600 to 600
- grad_top: bfloat16 [2, 2048, 1024], P(None, 'tm'), may hold values from -6 to 6
- w_in: bfloat16 [8, 1024, 3072], P('section'), may hold values from -0.1875 to 0.1875
- w_out: bfloat16 [8, 1024, 1024], P('section'), may hold values from -0.1875 to 0.1875
- offsets: int32 [32, 5], P('tm'), may hold values from 0 to 16, as said below
Outputs:
- d_acts: bfloat16 [8, 2, 2048, 1024], P('section', None, 'tm')
- d_w_in: float32 [8, 1024, 3072], P('section', 'tm')
- d_w_out: float32 [8, 1024, 1024], P('section', 'tm')
Inputs may be any that keep to these rules, and one draw needn't show every extreme that they name: offsets[t, k] is 0 or 2**k, and 0 wherever t < 2**k; the last shard uses every level.
All inputs are finite; a program needn't handle non-finite values.
Results may differ from a plain program's by a relative error of at most 0.018.
The roundings to bfloat16 on the way count: a program that leaves them out, or rounds other values in their place, can miss the bound.
Values may be sent and summed in bfloat16 or wider, within the bound.
A program may use at most 128 MiB of HBM per device.

v0:
```python
import jax
import jax.numpy as jnp
from jax import lax
from jax.sharding import PartitionSpec as P

HEAD_DIM = 64


epsilon = 1e-06
negative_fill = -1e30


def shifted(value, axis, steps):
    count = lax.axis_size(axis)
    initial, last = (max(0, -steps), min(count, count - steps))
    return lax.ppermute(value, axis, [(source, source + steps) for source in range(initial, last)])


def normalize(inputs):
    values = inputs.astype(jnp.float32)
    inverse_rms = lax.rsqrt(jnp.mean(values * values, axis=-1, keepdims=True) + epsilon)
    return (values * inverse_rms, inverse_rms)


def key_bias(level_flags, shard_rows):
    position = jnp.arange(shard_rows)
    own_part = position[None, :] <= position[:, None]
    far_part = jnp.repeat(level_flags != 0, shard_rows)
    far_part = jnp.broadcast_to(far_part[None, :], (shard_rows, far_part.shape[0]))
    return jnp.concatenate([own_part, far_part], 1)


def split_heads(row_block):
    return row_block.reshape(row_block.shape[0], -1, HEAD_DIM)


def softmax_keys(queries, key_heads, allowed):
    scores = jnp.einsum(
        "ihd,jhd->hij", queries, key_heads, preferred_element_type=jnp.float32
    ) * HEAD_DIM ** (-0.5)
    scores = jnp.where(allowed[None], scores, negative_fill)
    highest = jnp.max(scores, axis=-1, keepdims=True)
    shifted_exp = jnp.where(allowed[None], jnp.exp(scores - highest), 0.0)
    return shifted_exp / jnp.sum(shifted_exp, axis=-1, keepdims=True)


def attend(query_rows, key_rows, allowed):
    model_width = query_rows.shape[1]
    probability = softmax_keys(
        split_heads(query_rows), split_heads(key_rows[:, :model_width]), allowed
    )
    attended = jnp.einsum(
        "hij,jhd->ihd",
        probability.astype(jnp.bfloat16),
        split_heads(key_rows[:, model_width:]),
        preferred_element_type=jnp.float32,
    )
    return attended.reshape(query_rows.shape).astype(jnp.bfloat16)


def attend_back(query_rows, key_rows, allowed, incoming, attended, w_proj):
    model_width = query_rows.shape[1]
    queries = split_heads(query_rows)
    key_heads = split_heads(key_rows[:, :model_width])
    value_heads = split_heads(key_rows[:, model_width:])
    probability = softmax_keys(queries, key_heads, allowed)
    rounded = probability.astype(jnp.bfloat16)
    upstream = lax.dot_general(
        incoming, w_proj, (((1,), (1,)), ((), ())), preferred_element_type=jnp.float32
    ).astype(jnp.bfloat16)
    up_heads = split_heads(upstream)
    delta = jnp.einsum(
        "ihd,ihd->hi", up_heads.astype(jnp.float32), split_heads(attended).astype(jnp.float32)
    )[..., None]
    prob_grad = jnp.einsum(
        "ihd,jhd->hij", up_heads, value_heads, preferred_element_type=jnp.float32
    )
    score_grad = (probability * (prob_grad - delta)).astype(jnp.bfloat16)
    scale_factor = HEAD_DIM ** (-0.5)
    query_grad = (
        jnp.einsum("hij,jhd->ihd", score_grad, key_heads, preferred_element_type=jnp.float32)
        * scale_factor
    )
    key_grad = (
        jnp.einsum("hij,ihd->jhd", score_grad, queries, preferred_element_type=jnp.float32)
        * scale_factor
    )
    value_grad = jnp.einsum("hij,ihd->jhd", rounded, up_heads, preferred_element_type=jnp.float32)
    return (
        query_grad.reshape(-1, model_width),
        key_grad.reshape(-1, model_width),
        value_grad.reshape(-1, model_width),
    )


def per_device(acts, grad_top, w_in, w_out, offsets):
    sections = lax.axis_size("section")
    shards = lax.axis_size("tm")
    levels = shards.bit_length() - 1
    section_index = lax.axis_index("section")
    micro_count = acts.shape[1]
    shard_rows = acts.shape[2]
    model_width = acts.shape[3]
    w_qkv = w_in[0]
    w_proj = w_out[0]
    level_flags = offsets[0]
    normed, inverse_rms = normalize(acts[0])
    rounded_norm = normed.astype(jnp.bfloat16)
    qkv = jnp.dot(rounded_norm.reshape(-1, model_width), w_qkv, preferred_element_type=jnp.float32)
    qkv = qkv.astype(jnp.bfloat16).reshape(micro_count, shard_rows, 3 * model_width)
    pairs = qkv[..., model_width:]
    every_pair = lax.all_gather(pairs, "tm", axis=1, tiled=True)
    shard_index = lax.axis_index("tm")
    far_list = []
    for level in range(levels):
        source = jnp.maximum(shard_index - 2**level, 0) * shard_rows
        far_list.append(lax.dynamic_slice_in_dim(every_pair, source, shard_rows, 1))
    key_rows = jnp.concatenate([pairs] + far_list, 1)
    allowed = key_bias(level_flags, shard_rows)
    attended = jnp.stack(
        [
            attend(qkv[index, :, :model_width], key_rows[index], allowed)
            for index in range(micro_count)
        ],
        0,
    )

    def attention_part(incoming, slot):
        query_rows = lax.dynamic_index_in_dim(qkv, slot, 0, False)[:, :model_width]
        slot_keys = lax.dynamic_index_in_dim(key_rows, slot, 0, False)
        slot_attended = lax.dynamic_index_in_dim(attended, slot, 0, False)
        query_grad, key_grad, value_grad = attend_back(
            query_rows, slot_keys, allowed, incoming, slot_attended, w_proj
        )
        owner_sum = jnp.concatenate([key_grad[:shard_rows], value_grad[:shard_rows]], 1)
        far_part = jnp.concatenate([key_grad[shard_rows:], value_grad[shard_rows:]], 1)
        far_part = far_part.astype(jnp.bfloat16).reshape(levels, shard_rows, 2 * model_width)
        return (query_grad, owner_sum, far_part)

    def empty_attention(incoming, slot):
        return (
            jnp.zeros((shard_rows, model_width), jnp.float32),
            jnp.zeros((shard_rows, 2 * model_width), jnp.float32),
            jnp.zeros((levels, shard_rows, 2 * model_width), jnp.bfloat16),
        )

    def norm_part(qkv_grad, incoming, slot):
        norm_grad = lax.dot_general(
            qkv_grad, w_qkv, (((1,), (1,)), ((), ())), preferred_element_type=jnp.float32
        )
        slot_normed = lax.dynamic_index_in_dim(normed, slot, 0, False)
        slot_rms = lax.dynamic_index_in_dim(inverse_rms, slot, 0, False)
        inner = jnp.mean(norm_grad * slot_normed, axis=-1, keepdims=True)
        return (incoming.astype(jnp.float32) + slot_rms * (norm_grad - slot_normed * inner)).astype(
            jnp.bfloat16
        )

    def empty_norm(qkv_grad, incoming, slot):
        return jnp.zeros((shard_rows, model_width), jnp.bfloat16)

    def step(turn, carry):
        received, grad_store, qkv_store, incoming_store = carry
        slot_raw = turn - (sections - 1 - section_index)
        active = (slot_raw >= 0) & (slot_raw < micro_count)
        slot = jnp.clip(slot_raw, 0, micro_count - 1)
        incoming = jnp.where(
            section_index == sections - 1,
            lax.dynamic_index_in_dim(grad_top, slot, 0, False),
            received,
        )
        query_grad, owner_sum, far_part = lax.cond(
            active, attention_part, empty_attention, incoming, slot
        )
        for level in range(levels):
            owner_sum = owner_sum + shifted(far_part[level], "tm", -(2**level)).astype(jnp.float32)
        qkv_grad = jnp.concatenate([query_grad, owner_sum], 1).astype(jnp.bfloat16)
        grad_in = lax.cond(active, norm_part, empty_norm, qkv_grad, incoming, slot)
        sent_down = shifted(grad_in, "section", -1)
        grad_store = jnp.where(
            active, lax.dynamic_update_index_in_dim(grad_store, grad_in, slot, 0), grad_store
        )
        qkv_store = jnp.where(
            active, lax.dynamic_update_index_in_dim(qkv_store, qkv_grad, slot, 0), qkv_store
        )
        incoming_store = jnp.where(
            active,
            lax.dynamic_update_index_in_dim(incoming_store, incoming, slot, 0),
            incoming_store,
        )
        return (sent_down, grad_store, qkv_store, incoming_store)

    initial = (
        jnp.zeros((shard_rows, model_width), jnp.bfloat16),
        jnp.zeros((micro_count, shard_rows, model_width), jnp.bfloat16),
        jnp.zeros((micro_count, shard_rows, 3 * model_width), jnp.bfloat16),
        jnp.zeros((micro_count, shard_rows, model_width), jnp.bfloat16),
    )
    received, grad_store, qkv_store, incoming_store = lax.fori_loop(
        0, sections + micro_count - 1, step, initial
    )
    flat_norm = rounded_norm.reshape(-1, model_width)
    flat_attended = attended.reshape(-1, model_width)
    flat_qkv = qkv_store.reshape(-1, 3 * model_width)
    flat_incoming = incoming_store.reshape(-1, model_width)
    contract = (((0,), (0,)), ((), ()))
    first = lax.dot_general(flat_norm, flat_qkv, contract, preferred_element_type=jnp.float32)
    second = lax.dot_general(
        flat_attended, flat_incoming, contract, preferred_element_type=jnp.float32
    )
    summed = lax.psum_scatter(
        jnp.concatenate([first, second], 1).astype(jnp.bfloat16),
        "tm",
        scatter_dimension=0,
        tiled=True,
    ).astype(jnp.float32)
    return (
        grad_store[None],
        summed[None, :, : 3 * model_width],
        summed[None, :, 3 * model_width :],
    )


def solution(mesh):
    placed = (
        P("section", None, "tm", None),
        P(None, "tm", None),
        P("section", None, None),
        P("section", None, None),
        P("tm", None),
    )
    return jax.shard_map(
        per_device,
        mesh=mesh,
        in_specs=placed,
        out_specs=(
            P("section", None, "tm", None),
            P("section", "tm", None),
            P("section", "tm", None),
        ),
        check_vma=False,
    )
```

profile of v0, /device:TPU:2, one launch (start us, length us, event | category | flops | bytes accessed | tf_op | source)
XLA Modules:
  0.0 832.1 jit_solution(8413737208100853493)
XLA Ops:
  16.6 78.4 %all-gather.2.cloned.1.call-done = bf16[2,2048,2048]{2,1,0:T(8,128)(2,1)} async-done(((bf16[2,64,2048]{2,1,0:T(8,128)(2,1)}), bf16[2,2048,2048]{2,1,0:T(8,128)(2,1)}) %all-gather.2.cloned.1.call-update) | async-done | bytes 16777232 | tf_op jit(solution)/shard_map/all_gather | solution.py:112
  108.0 4.6 copy.45
  132.7 568.1 %while.21 = (s32[]{:T(128)}, bf16[64,1024]{1,0:T(8,128)(2,1)}, bf16[2,64,1024]{2,1,0:T(8,128)(2,1)}, bf16[2,64,3072]{2,1,0:T(8,128)(2,1)}, bf16[2,64,1024]{2,1,0...) while((s32[]{:T(128)}, bf16[64,1024]{1,0:T(8,128)(2,1)}, ...), condition=%wide.region_13.14_spmd, body=%wide.region_5.13_spmd.sunk | while | flops 800390528 | bytes 100328176 | solution.py:198
  148.2 4.9 collective-permute-done.1
  153.2 5.3 collective-permute-done.3
  220.0 4.4 collective-permute-done
  259.1 5.5 collective-permute-done.1
  296.2 5.3 collective-permute-done.1
  334.2 5.5 collective-permute-done.1
  348.6 4.8 collective-permute-done.5
  371.9 5.9 collective-permute-done.1
  385.1 189.5 %collective-permute-done.5 = bf16[64,1024]{1,0:T(8,128)(2,1)} collective-permute-done((bf16[64,1024]{1,0:T(8,128)(2,1)}, bf16[64,1024]{1,0:T(8,128)(2,1)}, u32[]{:S(2)}, u32[]{:S(2)}) %collective-permute-start.5) | collective-permute-done | bytes 131104 | tf_op jit(solution)/shard_map/while/body/eval_jaxpr/ppermute | solution.py:16
  576.3 22.1 %conditional.4 = (bf16[5,64,2048]{2,1,0:T(8,128)(2,1)S(1)}, f32[64,2048]{1,0:T(8,128)}, bf16[64,1024]{1,0:T(8,128)(2,1)S(1)}, bf16[1,64,1024]{2,1,0:T(8,128)(2,1)S(1)}) conditional(s32[]{:T(128)} %convert_element_type.218, () %tuple.93, (s32[]{:T(128)}, bf16[2,384,2048]{1,2,0:T(8,128)(2,1)}, pred[64,384]{1,0:T(8,128)(4,1)}, ...), branch_computations={%region_6.6_spmd, %region_7.9_spmd} | conditional | flops 393805184 | bytes 68079920 | solution.py:171
  614.4 5.5 collective-permute-done.1
  622.9 6.8 conditional.5
  622.9 5.1 fusion
  638.7 22.1 %conditional.4 = (bf16[5,64,2048]{2,1,0:T(8,128)(2,1)S(1)}, f32[64,2048]{1,0:T(8,128)}, bf16[64,1024]{1,0:T(8,128)(2,1)S(1)}, bf16[1,64,1024]{2,1,0:T(8,128)(2,1)S(1)}) conditional(s32[]{:T(128)} %convert_element_type.218, () %tuple.93, (s32[]{:T(128)}, bf16[2,384,2048]{1,2,0:T(8,128)(2,1)}, pred[64,384]{1,0:T(8,128)(4,1)}, ...), branch_computations={%region_6.6_spmd, %region_7.9_spmd} | conditional | flops 393805184 | bytes 68079920 | solution.py:171
  672.2 7.2 collective-permute-done
  679.5 5.6 collective-permute-done.1
  686.4 6.8 conditional.5
  686.4 5.1 fusion
  700.8 5.9 bitcast_convert_fusion
  708.3 6.9 pad_maximum_fusion.3
  715.2 107.6 %reduce-scatter.2.cloned.1.call-done = bf16[32,4096]{1,0:T(8,128)(2,1)} async-done(((bf16[1024,4096]{1,0:T(8,128)(2,1)}), bf16[32,4096]{1,0:T(8,128)(2,1)}) %reduce-scatter.2.cloned.1.call-update) | async-done | bytes 262160 | tf_op jit(solution)/shard_map/reduce_scatter | solution.py:210
  (393 shorter events, 365.2 us)
Async XLA Ops:
  7.2 87.9 %all-gather.2.cloned.1.call-start = ((), (), s32[]{:S(2)}) async-start(), calls=%async_computation.1 | async-start | bytes 17301504 | tf_op jit(solution)/shard_map/all_gather | solution.py:112
  14.3 808.5 %reduce-scatter.2.cloned.1.call-start = ((), (), s32[]{:S(2)}) async-start(), calls=%async_computation.2 | async-start | bytes 8650752 | tf_op jit(solution)/shard_map/reduce_scatter | solution.py:210
  136.9 16.2 %collective-permute-start.1 = (bf16[64,2048]{1,0:T(8,128)(2,1)S(1)}, bf16[64,2048]{1,0:T(8,128)(2,1)S(1)}, u32[]{:S(2)}, u32[]{:S(2)}) collective-permute-start(bf16[64,2048]{1,0:T(8,128)(2,1)S(1)} %get-tuple-element.615), channel_id=1, source_target_pairs={{8,0},{9,1},{10,2},{11,3},{12,4},{13,5},{14,6},{15,7},{16,8},{17,9... | collective-permute-start | bytes 786440 | tf_op jit(solution)/shard_map/while/body/eval_jaxpr/ppermute | solution.py:16
  174.6 16.4 %collective-permute-start.1 = (bf16[64,2048]{1,0:T(8,128)(2,1)S(1)}, bf16[64,2048]{1,0:T(8,128)(2,1)S(1)}, u32[]{:S(2)}, u32[]{:S(2)}) collective-permute-start(bf16[64,2048]{1,0:T(8,128)(2,1)S(1)} %get-tuple-element.615), channel_id=1, source_target_pairs={{8,0},{9,1},{10,2},{11,3},{12,4},{13,5},{14,6},{15,7},{16,8},{17,9... | collective-permute-start | bytes 786440 | tf_op jit(solution)/shard_map/while/body/eval_jaxpr/ppermute | solution.py:16
  178.5 16.0 %collective-permute-start.3 = (bf16[64,2048]{1,0:T(8,128)(2,1)S(1)}, bf16[64,2048]{1,0:T(8,128)(2,1)S(1)}, u32[]{:S(2)}, u32[]{:S(2)}) collective-permute-start(bf16[64,2048]{1,0:T(8,128)(2,1)S(1)} %get-tuple-element.617), channel_id=1, source_target_pairs={{2,0},{3,1},{4,2},{5,3},{6,4},{7,5},{8,6},{9,7},{10,8},{11,9},{12,... | collective-permute-start | bytes 786440 | tf_op jit(solution)/shard_map/while/body/eval_jaxpr/ppermute | solution.py:16
  180.4 16.3 %collective-permute-start.4 = (bf16[64,2048]{1,0:T(8,128)(2,1)S(1)}, bf16[64,2048]{1,0:T(8,128)(2,1)S(1)}, u32[]{:S(2)}, u32[]{:S(2)}) collective-permute-start(bf16[64,2048]{1,0:T(8,128)(2,1)S(1)} %get-tuple-element.619), channel_id=1, source_target_pairs={{1,0},{2,1},{3,2},{4,3},{5,4},{6,5},{7,6},{8,7},{9,8},{10,9},{11,1... | collective-permute-start | bytes 786440 | tf_op jit(solution)/shard_map/while/body/eval_jaxpr/ppermute | solution.py:16
  210.8 17.4 %collective-permute-start.1 = (bf16[64,2048]{1,0:T(8,128)(2,1)S(1)}, bf16[64,2048]{1,0:T(8,128)(2,1)S(1)}, u32[]{:S(2)}, u32[]{:S(2)}) collective-permute-start(bf16[64,2048]{1,0:T(8,128)(2,1)S(1)} %get-tuple-element.615), channel_id=1, source_target_pairs={{8,0},{9,1},{10,2},{11,3},{12,4},{13,5},{14,6},{15,7},{16,8},{17,9... | collective-permute-start | bytes 786440 | tf_op jit(solution)/shard_map/while/body/eval_jaxpr/ppermute | solution.py:16
  247.1 17.5 %collective-permute-start.1 = (bf16[64,2048]{1,0:T(8,128)(2,1)S(1)}, bf16[64,2048]{1,0:T(8,128)(2,1)S(1)}, u32[]{:S(2)}, u32[]{:S(2)}) collective-permute-start(bf16[64,2048]{1,0:T(8,128)(2,1)S(1)} %get-tuple-element.615), channel_id=1, source_target_pairs={{8,0},{9,1},{10,2},{11,3},{12,4},{13,5},{14,6},{15,7},{16,8},{17,9... | collective-permute-start | bytes 786440 | tf_op jit(solution)/shard_map/while/body/eval_jaxpr/ppermute | solution.py:16
  252.9 16.3 %collective-permute-start.4 = (bf16[64,2048]{1,0:T(8,128)(2,1)S(1)}, bf16[64,2048]{1,0:T(8,128)(2,1)S(1)}, u32[]{:S(2)}, u32[]{:S(2)}) collective-permute-start(bf16[64,2048]{1,0:T(8,128)(2,1)S(1)} %get-tuple-element.619), channel_id=1, source_target_pairs={{1,0},{2,1},{3,2},{4,3},{5,4},{6,5},{7,6},{8,7},{9,8},{10,9},{11,1... | collective-permute-start | bytes 786440 | tf_op jit(solution)/shard_map/while/body/eval_jaxpr/ppermute | solution.py:16
  283.9 17.5 %collective-permute-start.1 = (bf16[64,2048]{1,0:T(8,128)(2,1)S(1)}, bf16[64,2048]{1,0:T(8,128)(2,1)S(1)}, u32[]{:S(2)}, u32[]{:S(2)}) collective-permute-start(bf16[64,2048]{1,0:T(8,128)(2,1)S(1)} %get-tuple-element.615), channel_id=1, source_target_pairs={{8,0},{9,1},{10,2},{11,3},{12,4},{13,5},{14,6},{15,7},{16,8},{17,9... | collective-permute-start | bytes 786440 | tf_op jit(solution)/shard_map/while/body/eval_jaxpr/ppermute | solution.py:16
  289.7 16.3 %collective-permute-start.4 = (bf16[64,2048]{1,0:T(8,128)(2,1)S(1)}, bf16[64,2048]{1,0:T(8,128)(2,1)S(1)}, u32[]{:S(2)}, u32[]{:S(2)}) collective-permute-start(bf16[64,2048]{1,0:T(8,128)(2,1)S(1)} %get-tuple-element.619), channel_id=1, source_target_pairs={{1,0},{2,1},{3,2},{4,3},{5,4},{6,5},{7,6},{8,7},{9,8},{10,9},{11,1... | collective-permute-start | bytes 786440 | tf_op jit(solution)/shard_map/while/body/eval_jaxpr/ppermute | solution.py:16
  320.2 19.5 %collective-permute-start.1 = (bf16[64,2048]{1,0:T(8,128)(2,1)S(1)}, bf16[64,2048]{1,0:T(8,128)(2,1)S(1)}, u32[]{:S(2)}, u32[]{:S(2)}) collective-permute-start(bf16[64,2048]{1,0:T(8,128)(2,1)S(1)} %get-tuple-element.615), channel_id=1, source_target_pairs={{8,0},{9,1},{10,2},{11,3},{12,4},{13,5},{14,6},{15,7},{16,8},{17,9... | collective-permute-start | bytes 786440 | tf_op jit(solution)/shard_map/while/body/eval_jaxpr/ppermute | solution.py:16
  322.1 17.6 %collective-permute-start.2 = (bf16[64,2048]{1,0:T(8,128)(2,1)S(1)}, bf16[64,2048]{1,0:T(8,128)(2,1)S(1)}, u32[]{:S(2)}, u32[]{:S(2)}) collective-permute-start(bf16[64,2048]{1,0:T(8,128)(2,1)S(1)} %get-tuple-element.616), channel_id=1, source_target_pairs={{4,0},{5,1},{6,2},{7,3},{8,4},{9,5},{10,6},{11,7},{12,8},{13,9},{1... | collective-permute-start | bytes 786440 | tf_op jit(solution)/shard_map/while/body/eval_jaxpr/ppermute | solution.py:16
  357.7 20.1 %collective-permute-start.1 = (bf16[64,2048]{1,0:T(8,128)(2,1)S(1)}, bf16[64,2048]{1,0:T(8,128)(2,1)S(1)}, u32[]{:S(2)}, u32[]{:S(2)}) collective-permute-start(bf16[64,2048]{1,0:T(8,128)(2,1)S(1)} %get-tuple-element.615), channel_id=1, source_target_pairs={{8,0},{9,1},{10,2},{11,3},{12,4},{13,5},{14,6},{15,7},{16,8},{17,9... | collective-permute-start | bytes 786440 | tf_op jit(solution)/shard_map/while/body/eval_jaxpr/ppermute | solution.py:16
  359.6 18.2 %collective-permute-start.2 = (bf16[64,2048]{1,0:T(8,128)(2,1)S(1)}, bf16[64,2048]{1,0:T(8,128)(2,1)S(1)}, u32[]{:S(2)}, u32[]{:S(2)}) collective-permute-start(bf16[64,2048]{1,0:T(8,128)(2,1)S(1)} %get-tuple-element.616), channel_id=1, source_target_pairs={{4,0},{5,1},{6,2},{7,3},{8,4},{9,5},{10,6},{11,7},{12,8},{13,9},{1... | collective-permute-start | bytes 786440 | tf_op jit(solution)/shard_map/while/body/eval_jaxpr/ppermute | solution.py:16
  361.5 16.3 %collective-permute-start.3 = (bf16[64,2048]{1,0:T(8,128)(2,1)S(1)}, bf16[64,2048]{1,0:T(8,128)(2,1)S(1)}, u32[]{:S(2)}, u32[]{:S(2)}) collective-permute-start(bf16[64,2048]{1,0:T(8,128)(2,1)S(1)} %get-tuple-element.617), channel_id=1, source_target_pairs={{2,0},{3,1},{4,2},{5,3},{6,4},{7,5},{8,6},{9,7},{10,8},{11,9},{12,... | collective-permute-start | bytes 786440 | tf_op jit(solution)/shard_map/while/body/eval_jaxpr/ppermute | solution.py:16
  380.3 194.2 %collective-permute-start.5 = (bf16[64,1024]{1,0:T(8,128)(2,1)}, bf16[64,1024]{1,0:T(8,128)(2,1)}, u32[]{:S(2)}, u32[]{:S(2)}) collective-permute-start(bf16[64,1024]{1,0:T(8,128)(2,1)} %get-tuple-element.621), channel_id=1, source_target_pairs={{32,0},{64,32},{96,64},{128,96},{160,128},{192,160},{224,192},{33,... | collective-permute-start | bytes 393224 | tf_op jit(solution)/shard_map/while/body/eval_jaxpr/ppermute | solution.py:16
  599.9 20.0 %collective-permute-start.1 = (bf16[64,2048]{1,0:T(8,128)(2,1)S(1)}, bf16[64,2048]{1,0:T(8,128)(2,1)S(1)}, u32[]{:S(2)}, u32[]{:S(2)}) collective-permute-start(bf16[64,2048]{1,0:T(8,128)(2,1)S(1)} %get-tuple-element.615), channel_id=1, source_target_pairs={{8,0},{9,1},{10,2},{11,3},{12,4},{13,5},{14,6},{15,7},{16,8},{17,9... | collective-permute-start | bytes 786440 | tf_op jit(solution)/shard_map/while/body/eval_jaxpr/ppermute | solution.py:16
  601.8 18.1 %collective-permute-start.2 = (bf16[64,2048]{1,0:T(8,128)(2,1)S(1)}, bf16[64,2048]{1,0:T(8,128)(2,1)S(1)}, u32[]{:S(2)}, u32[]{:S(2)}) collective-permute-start(bf16[64,2048]{1,0:T(8,128)(2,1)S(1)} %get-tuple-element.616), channel_id=1, source_target_pairs={{4,0},{5,1},{6,2},{7,3},{8,4},{9,5},{10,6},{11,7},{12,8},{13,9},{1... | collective-permute-start | bytes 786440 | tf_op jit(solution)/shard_map/while/body/eval_jaxpr/ppermute | solution.py:16
  603.7 16.2 %collective-permute-start.3 = (bf16[64,2048]{1,0:T(8,128)(2,1)S(1)}, bf16[64,2048]{1,0:T(8,128)(2,1)S(1)}, u32[]{:S(2)}, u32[]{:S(2)}) collective-permute-start(bf16[64,2048]{1,0:T(8,128)(2,1)S(1)} %get-tuple-element.617), channel_id=1, source_target_pairs={{2,0},{3,1},{4,2},{5,3},{6,4},{7,5},{8,6},{9,7},{10,8},{11,9},{12,... | collective-permute-start | bytes 786440 | tf_op jit(solution)/shard_map/while/body/eval_jaxpr/ppermute | solution.py:16
  660.9 18.5 %collective-permute-start = (bf16[64,2048]{1,0:T(8,128)(2,1)S(1)}, bf16[64,2048]{1,0:T(8,128)(2,1)S(1)}, u32[]{:S(2)}, u32[]{:S(2)}) collective-permute-start(bf16[64,2048]{1,0:T(8,128)(2,1)S(1)} %get-tuple-element.614), channel_id=1, source_target_pairs={{16,0},{17,1},{18,2},{19,3},{20,4},{21,5},{22,6},{23,7},{24,8},{25... | collective-permute-start | bytes 786440 | tf_op jit(solution)/shard_map/while/body/eval_jaxpr/ppermute | solution.py:16
  662.2 22.8 %collective-permute-start.1 = (bf16[64,2048]{1,0:T(8,128)(2,1)S(1)}, bf16[64,2048]{1,0:T(8,128)(2,1)S(1)}, u32[]{:S(2)}, u32[]{:S(2)}) collective-permute-start(bf16[64,2048]{1,0:T(8,128)(2,1)S(1)} %get-tuple-element.615), channel_id=1, source_target_pairs={{8,0},{9,1},{10,2},{11,3},{12,4},{13,5},{14,6},{15,7},{16,8},{17,9... | collective-permute-start | bytes 786440 | tf_op jit(solution)/shard_map/while/body/eval_jaxpr/ppermute | solution.py:16
  664.2 20.9 %collective-permute-start.2 = (bf16[64,2048]{1,0:T(8,128)(2,1)S(1)}, bf16[64,2048]{1,0:T(8,128)(2,1)S(1)}, u32[]{:S(2)}, u32[]{:S(2)}) collective-permute-start(bf16[64,2048]{1,0:T(8,128)(2,1)S(1)} %get-tuple-element.616), channel_id=1, source_target_pairs={{4,0},{5,1},{6,2},{7,3},{8,4},{9,5},{10,6},{11,7},{12,8},{13,9},{1... | collective-permute-start | bytes 786440 | tf_op jit(solution)/shard_map/while/body/eval_jaxpr/ppermute | solution.py:16
  666.1 19.0 %collective-permute-start.3 = (bf16[64,2048]{1,0:T(8,128)(2,1)S(1)}, bf16[64,2048]{1,0:T(8,128)(2,1)S(1)}, u32[]{:S(2)}, u32[]{:S(2)}) collective-permute-start(bf16[64,2048]{1,0:T(8,128)(2,1)S(1)} %get-tuple-element.617), channel_id=1, source_target_pairs={{2,0},{3,1},{4,2},{5,3},{6,4},{7,5},{8,6},{9,7},{10,8},{11,9},{12,... | collective-permute-start | bytes 786440 | tf_op jit(solution)/shard_map/while/body/eval_jaxpr/ppermute | solution.py:16
  (69 other events, 772.6 us)
Sparse Core Ops, SparseCore 0:
  14.5 80.5 all-gather.1
  715.3 107.4 reduce-scatter.1
where the time goes:
time: 836 us; the launch traced here: 832 us
  waiting for transfers between devices  514 us (61%)
  starting transfers between devices  110 us (13%)
  local copies, waits for them, and re-layouts  74.5 us (9%)
  other arithmetic  72.8 us (9%)
  matrix products  44.7 us (5%)
  between operations  14.3 us (2%)
    ppermute x54, waiting for transfers between devices, shifted(): lax.ppermute(value, axis, [(source, source + steps) for source in range(i...  328 us
    ppermute x54, starting transfers between devices, shifted(): lax.ppermute(value, axis, [(source, source + steps) for source in range(i...  110 us
    reduce_scatter x1, waiting for transfers between devices, per_device(): lax.psum_scatter(jnp.concatenate([first, second], 1).astype(jnp.bfloat16)...  108 us
    all_gather x1, waiting for transfers between devices, per_device(): every_pair = lax.all_gather(pairs, 'tm', axis=1, tiled=True)  78.4 us
    select_n x9, other arithmetic, step(): jnp.where(active, lax.dynamic_update_index_in_dim(qkv_store, qkv_grad, sl...  16.7 us
  transfers between devices with their start and end apart: 56, of which 42 were waited for; matrix products, arithmetic and copies ran while one was open for 4% of the time, Pallas kernels for 0%

commit v1 on v0

v1 whole, which is shorter than its diff:
```python
import jax
import jax.numpy as jnp
from jax import lax
from jax.experimental import pallas as pl
from jax.experimental.pallas import tpu as pltpu
from jax.sharding import PartitionSpec as P

HEAD_DIM = 64
SCALE = HEAD_DIM ** (-0.5)
EPSILON = 1e-06
FILL = -1e30
MESH = pl.DeviceIdType.MESH

MB = 2
ROWS = 64
WIDTH = 1024
LEVELS = 5
BLOCKS = LEVELS + 1
KEYS = BLOCKS * ROWS
GROUP = 256
GROUPS = WIDTH // GROUP
CHUNK = 256
CHUNKS = WIDTH // CHUNK
PER = GROUP // HEAD_DIM

BF16 = jnp.bfloat16
F32 = jnp.float32


def dot(a, b):
    return lax.dot_general(a, b, (((1,), (0,)), ((), ())), preferred_element_type=F32)


def dot_nt(a, b):
    return lax.dot_general(a, b, (((1,), (1,)), ((), ())), preferred_element_type=F32)


def dot_tn(a, b):
    return lax.dot_general(a, b, (((0,), (0,)), ((), ())), preferred_element_type=F32)


def layer_kernel(
    sections,
    shards,
    acts_ref,
    gtop_ref,
    w_in_hbm,
    w_out_hbm,
    off_ref,
    dacts_ref,
    wg_ref,
    w_in,
    w_out,
    nall,
    normed,
    inv,
    qm,
    kv,
    p32,
    p16,
    bm,
    bias,
    inc,
    dq,
    part,
    att,
    ng,
    gsend,
    sbuf,
    rbuf,
    w_sem,
    fs,
    fr,
    bs,
    br,
    zs,
    zr,
):
    z = lax.axis_index("section")
    t = lax.axis_index("tm")
    steps = [2**level for level in range(LEVELS)]

    def up_shard(k):
        return lax.rem(t + steps[k], shards)

    def down_shard(k):
        return lax.rem(t + shards - steps[k], shards)

    copy_in = pltpu.make_async_copy(w_in_hbm, w_in, w_sem.at[0])
    copy_out = pltpu.make_async_copy(w_out_hbm, w_out, w_sem.at[1])
    copy_in.start()
    copy_out.start()

    barrier = pltpu.get_barrier_semaphore()
    for k in range(LEVELS):
        pl.semaphore_signal(barrier, inc=1, device_id=(z, up_shard(k)), device_id_type=MESH)
        if 2 * steps[k] != shards:
            pl.semaphore_signal(barrier, inc=1, device_id=(z, down_shard(k)), device_id_type=MESH)
    for step in (1, sections - 1):
        pl.semaphore_signal(
            barrier, inc=1, device_id=(lax.rem(z + step, sections), t), device_id_type=MESH
        )

    def fwd_copy(m, k):
        return pltpu.make_async_remote_copy(
            src_ref=nall.at[m, 0],
            dst_ref=nall.at[m, k + 1],
            send_sem=fs.at[m, k],
            recv_sem=fr.at[m, k],
            device_id=(z, up_shard(k)),
            device_id_type=MESH,
        )

    def bwd_copy(m, c, k):
        return pltpu.make_async_remote_copy(
            src_ref=sbuf.at[m, c, k],
            dst_ref=rbuf.at[m, c, k],
            send_sem=bs.at[m, c, k],
            recv_sem=br.at[m, c, k],
            device_id=(z, down_shard(k)),
            device_id_type=MESH,
        )

    def z_copy(m):
        return pltpu.make_async_remote_copy(
            src_ref=gsend.at[m],
            dst_ref=inc.at[m],
            send_sem=zs.at[m],
            recv_sem=zr.at[m],
            device_id=(lax.rem(z + sections - 1, sections), t),
            device_id_type=MESH,
        )

    for m in range(MB):
        x = acts_ref[m].astype(F32)
        inverse = lax.rsqrt(jnp.mean(x * x, axis=-1, keepdims=True) + EPSILON)
        value = x * inverse
        normed[m] = value
        inv[m] = jnp.broadcast_to(inverse, (ROWS, 128))
        nall[m, 0] = value.astype(BF16)
        for k in range(LEVELS):

            @pl.when(t < steps[k])
            def _():
                nall[m, k + 1] = jnp.zeros((ROWS, WIDTH), BF16)

    pl.semaphore_wait(barrier, 2 * LEVELS + 1)

    for m in range(MB):
        for k in reversed(range(LEVELS)):

            @pl.when(t + steps[k] < shards)
            def _():
                fwd_copy(m, k).start()

    row_head = lax.broadcasted_iota(jnp.int32, (GROUP, GROUP), 0) // HEAD_DIM
    lane_head = lax.broadcasted_iota(jnp.int32, (GROUP, GROUP), 1) // HEAD_DIM
    bm[...] = jnp.where(row_head == lane_head, 1.0, 0.0).astype(BF16)
    key_pos = lax.broadcasted_iota(jnp.int32, (ROWS, GROUP), 0)
    query_pos = lax.broadcasted_iota(jnp.int32, (ROWS, GROUP), 1) % ROWS
    bias[0:ROWS, :] = jnp.where(key_pos <= query_pos, 0.0, FILL)
    for k in range(LEVELS):
        fill = jnp.where(off_ref[0, k] != 0, 0.0, FILL)
        bias[(k + 1) * ROWS : (k + 2) * ROWS, :] = jnp.full((ROWS, GROUP), fill, F32)

    @pl.when(z == sections - 1)
    def _():
        inc[...] = gtop_ref[...]

    def spread(rows):
        return jnp.concatenate([rows] * PER, 0) * bm[...]

    def gather_heads(stacked):
        lanes = lax.broadcasted_iota(jnp.int32, (ROWS, GROUP), 1) // HEAD_DIM
        total = jnp.where(lanes == 0, stacked[0:ROWS], 0.0)
        for head in range(1, PER):
            total = jnp.where(lanes == head, stacked[head * ROWS : (head + 1) * ROWS], total)
        return total

    copy_in.wait()
    copy_out.wait()

    def own_query(c, carry):
        cols = pl.ds(pl.multiple_of(c * GROUP, GROUP), GROUP)
        both = jnp.concatenate([nall[0, 0], nall[1, 0]], 0)
        result = dot(both, w_in[:, cols]).astype(BF16)
        for m in range(MB):
            qm[m, c] = spread(result[m * ROWS : (m + 1) * ROWS])
        return carry

    lax.fori_loop(0, GROUPS, own_query, 0)

    def own_pair(c, carry):
        cols = pl.ds(pl.multiple_of(c * GROUP, GROUP), GROUP)
        source = pl.ds(pl.multiple_of(WIDTH + c * GROUP, GROUP), GROUP)
        both = jnp.concatenate([nall[0, 0], nall[1, 0]], 0)
        result = dot(both, w_in[:, source]).astype(BF16)
        for m in range(MB):
            kv[m, 0:ROWS, cols] = result[m * ROWS : (m + 1) * ROWS]
        return carry

    lax.fori_loop(0, 2 * GROUPS, own_pair, 0)

    def forward(m):
        for k in range(LEVELS):

            @pl.when(t >= steps[k])
            def _():
                fwd_copy(m, k).wait_recv()

        def far_pair(c, carry):
            cols = pl.ds(pl.multiple_of(c * GROUP, GROUP), GROUP)
            source = pl.ds(pl.multiple_of(WIDTH + c * GROUP, GROUP), GROUP)
            rows = nall[m, 1:BLOCKS].reshape(LEVELS * ROWS, WIDTH)
            kv[m, ROWS:KEYS, cols] = dot(rows, w_in[:, source]).astype(BF16)
            return carry

        lax.fori_loop(0, 2 * GROUPS, far_pair, 0)

        def probability(g, carry):
            cols = pl.ds(pl.multiple_of(g * GROUP, GROUP), GROUP)
            scores = dot_nt(kv[m, :, cols], qm[m, g]) * SCALE + bias[...]
            highest = jnp.max(scores, axis=0, keepdims=True)
            weights = jnp.exp(scores - highest)
            result = weights / jnp.sum(weights, axis=0, keepdims=True)
            p32[m, g] = result
            p16[m, g] = result.astype(BF16)
            return carry

        lax.fori_loop(0, GROUPS, probability, 0)

    def attend(m):
        def group(g, carry):
            cols = pl.ds(pl.multiple_of(g * GROUP, GROUP), GROUP)
            values = pl.ds(pl.multiple_of(WIDTH + g * GROUP, GROUP), GROUP)
            stacked = dot_tn(p16[m, g], kv[m, :, values])
            att[m * ROWS : (m + 1) * ROWS, cols] = gather_heads(stacked).astype(BF16)
            return carry

        lax.fori_loop(0, GROUPS, group, 0)

    def backward_send(m):
        @pl.when(z < sections - 1)
        def _():
            z_copy(m).wait_recv()

        def group(g, carry):
            cols = pl.ds(pl.multiple_of(g * GROUP, GROUP), GROUP)
            values = pl.ds(pl.multiple_of(WIDTH + g * GROUP, GROUP), GROUP)
            upstream = dot_nt(inc[m], w_out[cols, :]).astype(BF16)
            up_heads = spread(upstream)
            prob_grad = dot_nt(kv[m, :, values], up_heads)
            prob = p32[m, g]
            delta = jnp.sum(prob * prob_grad, axis=0, keepdims=True)
            score_grad = (prob * (prob_grad - delta)).astype(BF16)
            part[m, :, cols] = (dot(score_grad, qm[m, g]) * SCALE).astype(BF16)
            part[m, :, values] = dot(p16[m, g], up_heads).astype(BF16)
            stacked = dot_tn(score_grad, kv[m, :, cols])
            dq[m * ROWS : (m + 1) * ROWS, cols] = (gather_heads(stacked) * SCALE).astype(BF16)
            return carry

        lax.fori_loop(0, GROUPS, group, 0)

        def project(c, carry):
            cols = pl.ds(pl.multiple_of(c * CHUNK, CHUNK), CHUNK)
            result = dot_nt(part[m], w_in[cols, WIDTH : 3 * WIDTH])
            ng[m, :, cols] = result[0:ROWS]
            for k in reversed(range(LEVELS)):
                sbuf[m, c, k] = result[(k + 1) * ROWS : (k + 2) * ROWS].astype(BF16)

                @pl.when(t >= steps[k])
                def _():
                    bwd_copy(m, c, k).start()

            return carry

        lax.fori_loop(0, CHUNKS, project, 0)

        def own(c, carry):
            cols = pl.ds(pl.multiple_of(c * CHUNK, CHUNK), CHUNK)
            ng[m, :, cols] += dot_nt(dq[m * ROWS : (m + 1) * ROWS, :], w_in[cols, 0:WIDTH])
            return carry

        lax.fori_loop(0, CHUNKS, own, 0)

    def backward_finish(m):
        for c in range(CHUNKS):
            for k in range(LEVELS):

                @pl.when(t + steps[k] < shards)
                def _():
                    bwd_copy(m, c, k).wait_recv()
                    cols = slice(c * CHUNK, (c + 1) * CHUNK)
                    ng[m, :, cols] += rbuf[m, c, k].astype(F32)

        grad = ng[m]
        value = normed[m]
        inner = jnp.mean(grad * value, axis=-1, keepdims=True)
        result = (inc[m].astype(F32) + inv[m, :, 0:1] * (grad - value * inner)).astype(BF16)
        dacts_ref[m] = result
        gsend[m] = result

        @pl.when(z > 0)
        def _():
            z_copy(m).start()

    forward(0)
    backward_send(0)
    forward(1)
    attend(0)
    attend(1)
    backward_finish(0)
    backward_send(1)

    own_rows = jnp.concatenate([nall[0, 0], nall[1, 0]], 0)
    att_rows = att[...]
    inc_rows = inc[...].reshape(MB * ROWS, WIDTH)

    def weight(r, carry):
        rows = pl.ds(pl.multiple_of(r * CHUNK, CHUNK), CHUNK)
        far = nall[:, :, :, rows].reshape(MB * KEYS, CHUNK)
        own = jnp.concatenate([nall[0, 0, :, rows], nall[1, 0, :, rows]], 0)
        wg_ref[rows, 0:WIDTH] = dot_tn(own, dq[...]).astype(BF16)
        wg_ref[rows, WIDTH : 3 * WIDTH] = dot_tn(
            far, part[...].reshape(MB * KEYS, 2 * WIDTH)
        ).astype(BF16)
        wg_ref[rows, 3 * WIDTH : 4 * WIDTH] = dot_tn(
            att[:, rows], inc[...].reshape(MB * ROWS, WIDTH)
        ).astype(BF16)
        return carry

    lax.fori_loop(0, CHUNKS, weight, 0)
    backward_finish(1)

    for m in range(MB):
        for k in range(LEVELS):

            @pl.when(t + steps[k] < shards)
            def _():
                fwd_copy(m, k).wait_send()

            @pl.when(t >= steps[k])
            def _():
                for c in range(CHUNKS):
                    bwd_copy(m, c, k).wait_send()

        @pl.when(z > 0)
        def _():
            z_copy(m).wait_send()


def per_device(acts, grad_top, w_in, w_out, offsets):
    sections = lax.axis_size("section")
    shards = lax.axis_size("tm")
    import functools

    vmem = pl.BlockSpec(memory_space=pltpu.VMEM)
    d_acts, terms = pl.pallas_call(
        functools.partial(layer_kernel, sections, shards),
        out_shape=(
            jax.ShapeDtypeStruct((MB, ROWS, WIDTH), BF16),
            jax.ShapeDtypeStruct((WIDTH, 4 * WIDTH), BF16),
        ),
        in_specs=[
            vmem,
            vmem,
            pl.BlockSpec(memory_space=pl.ANY),
            pl.BlockSpec(memory_space=pl.ANY),
            pl.BlockSpec(memory_space=pltpu.SMEM),
        ],
        out_specs=(vmem, vmem),
        scratch_shapes=[
            pltpu.VMEM((WIDTH, 3 * WIDTH), BF16),
            pltpu.VMEM((WIDTH, WIDTH), BF16),
            pltpu.VMEM((MB, BLOCKS, ROWS, WIDTH), BF16),
            pltpu.VMEM((MB, ROWS, WIDTH), F32),
            pltpu.VMEM((MB, ROWS, 128), F32),
            pltpu.VMEM((MB, GROUPS, GROUP, GROUP), BF16),
            pltpu.VMEM((MB, KEYS, 2 * WIDTH), BF16),
            pltpu.VMEM((MB, GROUPS, KEYS, GROUP), F32),
            pltpu.VMEM((MB, GROUPS, KEYS, GROUP), BF16),
            pltpu.VMEM((GROUP, GROUP), BF16),
            pltpu.VMEM((KEYS, GROUP), F32),
            pltpu.VMEM((MB, ROWS, WIDTH), BF16),
            pltpu.VMEM((MB * ROWS, WIDTH), BF16),
            pltpu.VMEM((MB, KEYS, 2 * WIDTH), BF16),
            pltpu.VMEM((MB * ROWS, WIDTH), BF16),
            pltpu.VMEM((MB, ROWS, WIDTH), F32),
            pltpu.VMEM((MB, ROWS, WIDTH), BF16),
            pltpu.VMEM((MB, CHUNKS, LEVELS, ROWS, CHUNK), BF16),
            pltpu.VMEM((MB, CHUNKS, LEVELS, ROWS, CHUNK), BF16),
            pltpu.SemaphoreType.DMA((2,)),
            pltpu.SemaphoreType.DMA((MB, LEVELS)),
            pltpu.SemaphoreType.DMA((MB, LEVELS)),
            pltpu.SemaphoreType.DMA((MB, CHUNKS, LEVELS)),
            pltpu.SemaphoreType.DMA((MB, CHUNKS, LEVELS)),
            pltpu.SemaphoreType.DMA((MB,)),
            pltpu.SemaphoreType.DMA((MB,)),
        ],
        compiler_params=pltpu.CompilerParams(
            collective_id=0, has_side_effects=True, vmem_limit_bytes=60 * 1024 * 1024
        ),
        name="layer_kernel",
    )(acts[0], grad_top, w_in[0], w_out[0], offsets)
    summed = lax.psum_scatter(terms, "tm", scatter_dimension=0, tiled=True).astype(F32)
    return (d_acts[None], summed[None, :, : 3 * WIDTH], summed[None, :, 3 * WIDTH :])


def solution(mesh):
    placed = (
        P("section", None, "tm", None),
        P(None, "tm", None),
        P("section", None, None),
        P("section", None, None),
        P("tm", None),
    )
    return jax.shard_map(
        per_device,
        mesh=mesh,
        in_specs=placed,
        out_specs=(
            P("section", None, "tm", None),
            P("section", "tm", None),
            P("section", "tm", None),
        ),
        check_vma=False,
    )
```

time: 836 us -> 308 us (0.37)
  waiting for transfers between devices: 514 us -> 96 us
  Pallas kernels: 0 us -> 195 us
  starting transfers between devices: 110 us -> 0.04 us
  local copies, waits for them, and re-layouts: 74.5 us -> 2.14 us
  other arithmetic: 72.8 us -> 0.98 us
  matrix products: 44.7 us -> 0 us
    ppermute x54 -> x0, waiting for transfers between devices: 328 us -> none  [shifted(): lax.ppermute(value, axis, [(source, source + steps) for source in range(i...]
    pallas_call x0 -> x1, Pallas kernels: none -> 195 us  [per_device(): pl.pallas_call(functools.partial(layer_kernel, sections, shards), out_sha...]
    ppermute x54 -> x0, starting transfers between devices: 110 us -> none  [shifted(): lax.ppermute(value, axis, [(source, source + steps) for source in range(i...]
    all_gather x1 -> x0, waiting for transfers between devices: 78.4 us -> none  [per_device(): every_pair = lax.all_gather(pairs, 'tm', axis=1, tiled=True)]
    select_n x27 -> x0, other arithmetic: 46.7 us -> none  [the longest x9 16.7 us: step(): jnp.where(active, lax.dynamic_update_index_in_dim(qkv_store, qkv_grad, sl...]
    dot_general x17 -> x0, matrix products: 33.6 us -> none  [the longest x2 10.2 us: norm_part(): lax.dot_general(qkv_grad, w_qkv, (((1,), (1,)), ((), ())), preferred_elem...]
    slice x23 -> x0, local copies, waits for them, and re-layouts: 18.1 us -> none  [the longest x3 5.65 us: attend(): key_rows[:, :model_width]]
    another operation x33 -> x0, local copies, waits for them, and re-layouts: 14 us -> none
  transfers between devices with their start and end apart: 56 -> 1, of which waited for: 42 -> 1; matrix products, arithmetic and copies ran while one was open for 4% -> 0% of each run, Pallas kernels for 0% -> 0%
where the time goes in v1:
time: 308 us
  Pallas kernels  195 us (63%)
  waiting for transfers between devices  96 us (31%)
  between operations  14 us (5%)
    pallas_call x1, Pallas kernels, per_device(): pl.pallas_call(functools.partial(layer_kernel, sections, shards), out_sha...  195 us
    reduce_scatter x1, waiting for transfers between devices, per_device(): lax.psum_scatter(terms, 'tm', scatter_dimension=0, tiled=True).astype(F32)  96 us
  transfers between devices with their start and end apart: 1, of which 1 were waited for; matrix products, arithmetic and copies ran while one was open for 0% of the time, Pallas kernels for 0%

profile of v1, /device:TPU:2, one launch (start us, length us, event | category | flops | bytes accessed | tf_op | source)
XLA Modules:
  0.0 308.1 jit_solution(15316191085663756161)
XLA Ops:
  7.2 0.0 reduce-scatter.2.cloned.1.call-start
  7.2 195.0 %layer_kernel.1 = (bf16[2,64,1024]{2,1,0:T(8,128)(2,1)}, bf16[1024,4096]{1,0:T(8,128)(2,1)}) custom-call(bf16[2,64,1024]{2,1,0:T(8,128)(2,1)} %bitcast.10, bf16[2,64,1024]{2,1,0:T(8,128)(2,1)} %gtop_ref.1, bf16[1024,3072]{1,0:T(8,128)(2,1)} %bitcast.8, bf16[1024,1024]{1,0:T(8,128)(2,1)} %bitcast.9, s32[1,5]{1,0:T(1,128)} %off_ref.1), custom_call_target="tpu_custom_call" | custom-call | tf_op jit(solution)/shard_map/layer_kernel/pallas_call | solution.py:358
  202.2 0.0 copy-start
  202.2 0.0 reduce-scatter.2.cloned.1.call-update
  202.2 96.0 %reduce-scatter.2.cloned.1.call-done = bf16[32,4096]{1,0:T(8,128)(2,1)} async-done(((bf16[1024,4096]{1,0:T(8,128)(2,1)}), bf16[32,4096]{1,0:T(8,128)(2,1)}) %reduce-scatter.2.cloned.1.call-update) | async-done | bytes 262160 | tf_op jit(solution)/shard_map/reduce_scatter | solution.py:405
  298.2 1.0 convert_element_type.3
  299.2 0.7 slice_bitcast_fusion.1
  299.8 0.8 slice_bitcast_fusion
  300.6 0.0 copy-done
  300.6 0.7 copy.9
Async XLA Ops:
  7.2 291.0 %reduce-scatter.2.cloned.1.call-start = ((), (), s32[]{:S(2)}) async-start(), calls=%async_computation.1 | async-start | bytes 8650752 | tf_op jit(solution)/shard_map/reduce_scatter | solution.py:405
  202.2 98.4 %copy-start = (bf16[2,64,1024]{2,1,0:T(8,128)(2,1)S(1)}, bf16[2,64,1024]{2,1,0:T(8,128)(2,1)}, u32[]{:S(2)}) copy-start(bf16[2,64,1024]{2,1,0:T(8,128)(2,1)} %get-tuple-element.5) | copy-start | bytes 786436
Sparse Core Ops, SparseCore 0:
  202.3 95.7 reduce-scatter.1

commit v2 on v1

--- a/solution.py
+++ b/solution.py
@@ -1,3 +1,5 @@
+import functools
+
 import jax
 import jax.numpy as jnp
 from jax import lax
@@ -22,6 +24,11 @@
 CHUNK = 256
 CHUNKS = WIDTH // CHUNK
 PER = GROUP // HEAD_DIM
+SIDE = 4
+SLICE = 32
+PARTS = 8
+COLS = 512
+HALF = COLS // 2
 
 BF16 = jnp.bfloat16
 F32 = jnp.float32
@@ -48,7 +55,8 @@
     w_out_hbm,
     off_ref,
     dacts_ref,
-    wg_ref,
+    dwin_ref,
+    dwout_ref,
     w_in,
     w_out,
     nall,
@@ -75,10 +83,44 @@
     br,
     zs,
     zr,
+    n_t,
+    own_t,
+    att_t,
+    psend,
+    precv,
+    total,
+    send1,
+    recv1,
+    send2,
+    recv2,
+    column,
+    send3,
+    recv3,
+    send4,
+    recv4,
+    ps,
+    pr,
+    s1,
+    r1,
+    s2,
+    r2,
+    s3,
+    r3,
+    s4,
+    r4,
 ):
     z = lax.axis_index("section")
     t = lax.axis_index("tm")
     steps = [2**level for level in range(LEVELS)]
+    place_x = t // 8
+    place_y = lax.rem(t // 2, SIDE)
+    core = lax.rem(t, 2)
+    partner = t + 1 - 2 * core
+
+    def along(axis, step):
+        if axis == 0:
+            return lax.rem(t + 8 * (step % SIDE), shards)
+        return place_x * 8 + lax.rem(place_y + step % SIDE, SIDE) * 2 + core
 
     def up_shard(k):
         return lax.rem(t + steps[k], shards)
@@ -96,6 +138,8 @@
         pl.semaphore_signal(barrier, inc=1, device_id=(z, up_shard(k)), device_id_type=MESH)
         if 2 * steps[k] != shards:
             pl.semaphore_signal(barrier, inc=1, device_id=(z, down_shard(k)), device_id_type=MESH)
+    for peer in (along(1, 1), along(1, -1), partner):
+        pl.semaphore_signal(barrier, inc=1, device_id=(z, peer), device_id_type=MESH)
     for step in (1, sections - 1):
         pl.semaphore_signal(
             barrier, inc=1, device_id=(lax.rem(z + step, sections), t), device_id_type=MESH
@@ -144,7 +188,7 @@
             def _():
                 nall[m, k + 1] = jnp.zeros((ROWS, WIDTH), BF16)
 
-    pl.semaphore_wait(barrier, 2 * LEVELS + 1)
+    pl.semaphore_wait(barrier, 2 * LEVELS + 4)
 
     for m in range(MB):
         for k in reversed(range(LEVELS)):
@@ -304,33 +348,177 @@
         def _():
             z_copy(m).start()
 
+    def remote(src, dst, send_sem, recv_sem, peer):
+        return pltpu.make_async_remote_copy(
+            src_ref=src,
+            dst_ref=dst,
+            send_sem=send_sem,
+            recv_sem=recv_sem,
+            device_id=(z, peer),
+            device_id_type=MESH,
+        )
+
+    def pair_copy(i):
+        return remote(psend.at[i], precv.at[i], ps.at[i], pr.at[i], partner)
+
+    def ring_copy(stage, i, side):
+        send, recv, ss, rs = ring_refs[stage]
+        axis = (i + stage // 2) % 2
+        return remote(
+            send.at[i, side],
+            recv.at[i, side],
+            ss.at[i, side],
+            rs.at[i, side],
+            along(axis, 1 if side == 0 else -1),
+        )
+
+    ring_refs = (
+        (send1, recv1, s1, r1),
+        (send2, recv2, s2, r2),
+        (send3, recv3, s3, r3),
+        (send4, recv4, s4, r4),
+    )
+
+    def transpose_rows():
+        def block(r, carry):
+            rows = pl.ds(pl.multiple_of(r * CHUNK, CHUNK), CHUNK)
+            owns = []
+            for m in range(MB):
+                tokens = nall[m, :, :, rows].reshape(KEYS, CHUNK)
+                turned = tokens.T.reshape(SIDE, 2, SLICE, KEYS)
+                for parity in range(2):
+                    n_t[parity, r, :, :, m * KEYS : (m + 1) * KEYS] = turned[:, parity]
+                owns.append(nall[m, 0, :, rows])
+            turned = jnp.concatenate(owns, 0).T.reshape(SIDE, 2, SLICE, MB * ROWS)
+            turned_att = att[:, rows].T.reshape(SIDE, 2, SLICE, MB * ROWS)
+            for parity in range(2):
+                own_t[parity, r] = turned[:, parity]
+                att_t[parity, r] = turned_att[:, parity]
+            return carry
+
+        lax.fori_loop(0, SIDE, block, 0)
+
+    def operands(i):
+        if i < 2:
+            return own_t, dq[:, i * COLS : (i + 1) * COLS], i * COLS
+        if i < 4:
+            low = (i - 2) * COLS
+            return (
+                att_t,
+                inc[:, :, low : low + COLS].reshape(MB * ROWS, COLS),
+                3 * WIDTH + low,
+            )
+        low = (i - 4) * COLS
+        return n_t, part[:, :, low : low + COLS].reshape(MB * KEYS, COLS), WIDTH + low
+
+    def weight_part(i):
+        left, right, _ = operands(i)
+        depth = right.shape[0]
+        shape = (SIDE, SIDE, SLICE, COLS)
+        away = left[1 - core].reshape(WIDTH // 2, depth)
+        psend[i] = dot(away, right).astype(BF16).reshape(shape)
+        pair_copy(i).start()
+        here = left[core].reshape(WIDTH // 2, depth)
+        total[i] = dot(here, right).reshape(shape)
+
+    def pick(i, step):
+        axis = i % 2
+        where = lax.rem((place_x if axis == 0 else place_y) + step % SIDE, SIDE)
+        return total[i, where] if axis == 0 else total[i, :, where]
+
+    def pick_row(i, step):
+        axis = (i + 1) % 2
+        return column[i, lax.rem((place_x if axis == 0 else place_y) + step % SIDE, SIDE)]
+
+    def ring_one(i):
+        pair_copy(i).wait_recv()
+        total[i] += precv[i].astype(F32)
+        far = pick(i, 2).astype(BF16)
+        send1[i, 0] = far[:, :, :HALF]
+        send1[i, 1] = far[:, :, HALF:]
+        for side in range(2):
+            ring_copy(0, i, side).start()
+
+    def ring_two(i):
+        for side in range(2):
+            ring_copy(0, i, side).wait_recv()
+        right, left = pick(i, 1), pick(i, -1)
+        send2[i, 0, :, :, :HALF] = (right[:, :, :HALF] + recv1[i, 0].astype(F32)).astype(BF16)
+        send2[i, 0, :, :, HALF:] = right[:, :, HALF:].astype(BF16)
+        ring_copy(1, i, 0).start()
+        send2[i, 1, :, :, :HALF] = left[:, :, :HALF].astype(BF16)
+        send2[i, 1, :, :, HALF:] = (left[:, :, HALF:] + recv1[i, 1].astype(F32)).astype(BF16)
+        ring_copy(1, i, 1).start()
+
+    def ring_three(i):
+        for side in range(2):
+            ring_copy(1, i, side).wait_recv()
+        column[i] = pick(i, 0) + recv2[i, 0].astype(F32) + recv2[i, 1].astype(F32)
+        far = pick_row(i, 2).astype(BF16)
+        send3[i, 0] = far[:, :HALF]
+        send3[i, 1] = far[:, HALF:]
+        for side in range(2):
+            ring_copy(2, i, side).start()
+
+    def ring_four(i):
+        for side in range(2):
+            ring_copy(2, i, side).wait_recv()
+        right, left = pick_row(i, 1), pick_row(i, -1)
+        send4[i, 0, :, :HALF] = (right[:, :HALF] + recv3[i, 0].astype(F32)).astype(BF16)
+        send4[i, 0, :, HALF:] = right[:, HALF:].astype(BF16)
+        ring_copy(3, i, 0).start()
+        send4[i, 1, :, :HALF] = left[:, :HALF].astype(BF16)
+        send4[i, 1, :, HALF:] = (left[:, HALF:] + recv3[i, 1].astype(F32)).astype(BF16)
+        ring_copy(3, i, 1).start()
+
+    def ring_last(i):
+        for side in range(2):
+            ring_copy(3, i, side).wait_recv()
+        result = pick_row(i, 0) + recv4[i, 0].astype(F32) + recv4[i, 1].astype(F32)
+        low = operands(i)[2]
+        if low < 3 * WIDTH:
+            dwin_ref[:, low : low + COLS] = result
+        else:
+            dwout_ref[:, low - 3 * WIDTH : low - 3 * WIDTH + COLS] = result
+
     forward(0)
     backward_send(0)
     forward(1)
     attend(0)
     attend(1)
     backward_finish(0)
+    transpose_rows()
     backward_send(1)
 
-    own_rows = jnp.concatenate([nall[0, 0], nall[1, 0]], 0)
-    att_rows = att[...]
-    inc_rows = inc[...].reshape(MB * ROWS, WIDTH)
-
-    def weight(r, carry):
-        rows = pl.ds(pl.multiple_of(r * CHUNK, CHUNK), CHUNK)
-        far = nall[:, :, :, rows].reshape(MB * KEYS, CHUNK)
-        own = jnp.concatenate([nall[0, 0, :, rows], nall[1, 0, :, rows]], 0)
-        wg_ref[rows, 0:WIDTH] = dot_tn(own, dq[...]).astype(BF16)
-        wg_ref[rows, WIDTH : 3 * WIDTH] = dot_tn(
-            far, part[...].reshape(MB * KEYS, 2 * WIDTH)
-        ).astype(BF16)
-        wg_ref[rows, 3 * WIDTH : 4 * WIDTH] = dot_tn(
-            att[:, rows], inc[...].reshape(MB * ROWS, WIDTH)
-        ).astype(BF16)
-        return carry
-
-    lax.fori_loop(0, CHUNKS, weight, 0)
-    backward_finish(1)
+    @pl.when(z > 0)
+    def _():
+        backward_finish(1)
+
+    for i in range(PARTS + 1):
+        if i < PARTS:
+            weight_part(i)
+        if i >= 1:
+            ring_one(i - 1)
+
+    @pl.when(z == 0)
+    def _():
+        backward_finish(1)
+
+    for i in range(PARTS + 3):
+        if i < PARTS:
+            ring_two(i)
+        if 1 <= i <= PARTS:
+            ring_three(i - 1)
+        if 2 <= i <= PARTS + 1:
+            ring_four(i - 2)
+        if i >= 3:
+            ring_last(i - 3)
+
+    for i in range(PARTS):
+        pair_copy(i).wait_send()
+        for stage in range(4):
+            for side in range(2):
+                ring_copy(stage, i, side).wait_send()
 
     for m in range(MB):
         for k in range(LEVELS):
@@ -352,14 +540,13 @@
 def per_device(acts, grad_top, w_in, w_out, offsets):
     sections = lax.axis_size("section")
     shards = lax.axis_size("tm")
-    import functools
-
     vmem = pl.BlockSpec(memory_space=pltpu.VMEM)
-    d_acts, terms = pl.pallas_call(
+    d_acts, d_in, d_out = pl.pallas_call(
         functools.partial(layer_kernel, sections, shards),
         out_shape=(
             jax.ShapeDtypeStruct((MB, ROWS, WIDTH), BF16),
-            jax.ShapeDtypeStruct((WIDTH, 4 * WIDTH), BF16),
+            jax.ShapeDtypeStruct((SLICE, 3 * WIDTH), F32),
+            jax.ShapeDtypeStruct((SLICE, WIDTH), F32),
         ),
         in_specs=[
             vmem,
@@ -368,7 +555,7 @@
             pl.BlockSpec(memory_space=pl.ANY),
             pl.BlockSpec(memory_space=pltpu.SMEM),
         ],
-        out_specs=(vmem, vmem),
+        out_specs=(vmem, vmem, vmem),
         scratch_shapes=[
             pltpu.VMEM((WIDTH, 3 * WIDTH), BF16),
             pltpu.VMEM((WIDTH, WIDTH), BF16),
@@ -396,14 +583,31 @@
             pltpu.SemaphoreType.DMA((MB, CHUNKS, LEVELS)),
             pltpu.SemaphoreType.DMA((MB,)),
             pltpu.SemaphoreType.DMA((MB,)),
-        ],
+            pltpu.VMEM((2, SIDE, SIDE, SLICE, MB * KEYS), BF16),
+            pltpu.VMEM((2, SIDE, SIDE, SLICE, MB * ROWS), BF16),
+            pltpu.VMEM((2, SIDE, SIDE, SLICE, MB * ROWS), BF16),
+            pltpu.VMEM((PARTS, SIDE, SIDE, SLICE, COLS), BF16),
+            pltpu.VMEM((PARTS, SIDE, SIDE, SLICE, COLS), BF16),
+            pltpu.VMEM((PARTS, SIDE, SIDE, SLICE, COLS), F32),
+            pltpu.VMEM((PARTS, 2, SIDE, SLICE, HALF), BF16),
+            pltpu.VMEM((PARTS, 2, SIDE, SLICE, HALF), BF16),
+            pltpu.VMEM((PARTS, 2, SIDE, SLICE, COLS), BF16),
+            pltpu.VMEM((PARTS, 2, SIDE, SLICE, COLS), BF16),
+            pltpu.VMEM((PARTS, SIDE, SLICE, COLS), F32),
+            pltpu.VMEM((PARTS, 2, SLICE, HALF), BF16),
+            pltpu.VMEM((PARTS, 2, SLICE, HALF), BF16),
+            pltpu.VMEM((PARTS, 2, SLICE, COLS), BF16),
+            pltpu.VMEM((PARTS, 2, SLICE, COLS), BF16),
+            pltpu.SemaphoreType.DMA((PARTS,)),
+            pltpu.SemaphoreType.DMA((PARTS,)),
+        ]
+        + [pltpu.SemaphoreType.DMA((PARTS, 2))] * 8,
         compiler_params=pltpu.CompilerParams(
-            collective_id=0, has_side_effects=True, vmem_limit_bytes=60 * 1024 * 1024
+            collective_id=0, has_side_effects=True, vmem_limit_bytes=63 * 1024 * 1024
         ),
         name="layer_kernel",
     )(acts[0], grad_top, w_in[0], w_out[0], offsets)
-    summed = lax.psum_scatter(terms, "tm", scatter_dimension=0, tiled=True).astype(F32)
-    return (d_acts[None], summed[None, :, : 3 * WIDTH], summed[None, :, 3 * WIDTH :])
+    return (d_acts[None], d_in[None], d_out[None])
 
 
 def solution(mesh):

time: 308 us -> 241 us (0.78)
  waiting for transfers between devices: 96 us -> 0 us
  Pallas kernels: 195 us -> 235 us
  between operations: 14 us -> 0.64 us
    reduce_scatter x1 -> x0, waiting for transfers between devices: 96 us -> none  [per_device(): lax.psum_scatter(terms, 'tm', scatter_dimension=0, tiled=True).astype(F32)]
    pallas_call x1, Pallas kernels: 195 us -> 235 us  [per_device(): pl.pallas_call(functools.partial(layer_kernel, sections, shards), out_sha...]
    unnamed x3, local copies, waits for them, and re-layouts: 0.71 us -> 5 us
  transfers between devices with their start and end apart: 1 -> 0, of which waited for: 1 -> 0; matrix products, arithmetic and copies ran while one was open for 0% -> 0% of each run, Pallas kernels for 0% -> 0%
where the time goes in v2:
time: 241 us
  Pallas kernels  235 us (98%)
  local copies, waits for them, and re-layouts  5 us (2%)
    pallas_call x1, Pallas kernels, per_device(): pl.pallas_call(functools.partial(layer_kernel, sections, shards), out_sha...  235 us
    unnamed x3, local copies, waits for them, and re-layouts  5 us

profile of v2, /device:TPU:2, one launch (start us, length us, event | category | flops | bytes accessed | tf_op | source)
XLA Modules:
  0.0 240.5 jit_solution(4713852827461474423)
XLA Ops:
  0.6 234.9 %layer_kernel.1 = (bf16[2,64,1024]{2,1,0:T(8,128)(2,1)}, f32[32,3072]{1,0:T(8,128)}, f32[32,1024]{1,0:T(8,128)}) custom-call(bf16[2,64,1024]{2,1,0:T(8,128)(2,1)} %bitcast.9, bf16[2,64,1024]{2,1,0:T(8,128)(2,1)} %gtop_ref.1, bf16[1024,3072]{1,0:T(8,128)(2,1)} %bitcast.6, bf16[1024,1024]{1,0:T(8,128)(2,1)} %bitcast.7, s32[1,5]{1,0:T(1,128)} %off_ref.1), custom_call_target="tpu_custom_call" | custom-call | tf_op jit(solution)/shard_map/layer_kernel/pallas_call | solution.py:544
  235.5 1.7 copy.11
  237.2 1.8 copy.12
  239.0 1.6 copy.13

commit v3 on v2

--- a/solution.py
+++ b/solution.py
@@ -108,6 +108,9 @@
     r3,
     s4,
     r4,
+    sg,
+    up32,
+    up16,
 ):
     z = lax.axis_index("section")
     t = lax.axis_index("tm")
@@ -165,12 +168,13 @@
             device_id_type=MESH,
         )
 
-    def z_copy(m):
+    def z_copy(m, h):
+        cols = pl.ds(h * COLS, COLS)
         return pltpu.make_async_remote_copy(
-            src_ref=gsend.at[m],
-            dst_ref=inc.at[m],
-            send_sem=zs.at[m],
-            recv_sem=zr.at[m],
+            src_ref=gsend.at[m, :, cols],
+            dst_ref=inc.at[m, :, cols],
+            send_sem=zs.at[m, h],
+            recv_sem=zr.at[m, h],
             device_id=(lax.rem(z + sections - 1, sections), t),
             device_id_type=MESH,
         )
@@ -182,20 +186,19 @@
         normed[m] = value
         inv[m] = jnp.broadcast_to(inverse, (ROWS, 128))
         nall[m, 0] = value.astype(BF16)
+        if m == 0:
+            pl.semaphore_wait(barrier, 2 * LEVELS + 4)
+        for k in reversed(range(LEVELS)):
+
+            @pl.when(t + steps[k] < shards)
+            def _():
+                fwd_copy(m, k).start()
+
         for k in range(LEVELS):
 
             @pl.when(t < steps[k])
             def _():
                 nall[m, k + 1] = jnp.zeros((ROWS, WIDTH), BF16)
-
-    pl.semaphore_wait(barrier, 2 * LEVELS + 4)
-
-    for m in range(MB):
-        for k in reversed(range(LEVELS)):
-
-            @pl.when(t + steps[k] < shards)
-            def _():
-                fwd_copy(m, k).start()
 
     row_head = lax.broadcasted_iota(jnp.int32, (GROUP, GROUP), 0) // HEAD_DIM
     lane_head = lax.broadcasted_iota(jnp.int32, (GROUP, GROUP), 1) // HEAD_DIM
@@ -259,7 +262,7 @@
             kv[m, ROWS:KEYS, cols] = dot(rows, w_in[:, source]).astype(BF16)
             return carry
 
-        lax.fori_loop(0, 2 * GROUPS, far_pair, 0)
+        lax.fori_loop(0, 2 * GROUPS, far_pair, 0, unroll=2)
 
         def probability(g, carry):
             cols = pl.ds(pl.multiple_of(g * GROUP, GROUP), GROUP)
@@ -271,7 +274,7 @@
             p16[m, g] = result.astype(BF16)
             return carry
 
-        lax.fori_loop(0, GROUPS, probability, 0)
+        lax.fori_loop(0, GROUPS, probability, 0, unroll=True)
 
     def attend(m):
         def group(g, carry):
@@ -283,34 +286,57 @@
 
         lax.fori_loop(0, GROUPS, group, 0)
 
-    def backward_send(m):
-        @pl.when(z < sections - 1)
+    def wait_incoming(m, h):
+        z_copy(m, h).wait_recv()
+
+    def stage_upstream(m):
+        waits = (z < sections - 1) if m == 0 else (z < sections - 1) & (z > 0)
+
+        @pl.when(waits)
         def _():
-            z_copy(m).wait_recv()
-
+            wait_incoming(m, 0)
+
+        def first(g, carry):
+            cols = pl.ds(pl.multiple_of(g * GROUP, GROUP), GROUP)
+            up32[:, cols] = dot_nt(inc[m, :, 0:COLS], w_out[cols, 0:COLS])
+            return carry
+
+        lax.fori_loop(0, GROUPS, first, 0, unroll=True)
+
+        @pl.when(waits)
+        def _():
+            wait_incoming(m, 1)
+
+        def second(g, carry):
+            cols = pl.ds(pl.multiple_of(g * GROUP, GROUP), GROUP)
+            rest = dot_nt(inc[m, :, COLS : 2 * COLS], w_out[cols, COLS : 2 * COLS])
+            up16[:, cols] = (up32[:, cols] + rest).astype(BF16)
+            return carry
+
+        lax.fori_loop(0, GROUPS, second, 0, unroll=True)
+
+    def stage_parts(m):
         def group(g, carry):
             cols = pl.ds(pl.multiple_of(g * GROUP, GROUP), GROUP)
             values = pl.ds(pl.multiple_of(WIDTH + g * GROUP, GROUP), GROUP)
-            upstream = dot_nt(inc[m], w_out[cols, :]).astype(BF16)
-            up_heads = spread(upstream)
+            up_heads = spread(up16[:, cols])
             prob_grad = dot_nt(kv[m, :, values], up_heads)
+            part[m, :, values] = dot(p16[m, g], up_heads).astype(BF16)
             prob = p32[m, g]
             delta = jnp.sum(prob * prob_grad, axis=0, keepdims=True)
             score_grad = (prob * (prob_grad - delta)).astype(BF16)
+            sg[g] = score_grad
             part[m, :, cols] = (dot(score_grad, qm[m, g]) * SCALE).astype(BF16)
-            part[m, :, values] = dot(p16[m, g], up_heads).astype(BF16)
-            stacked = dot_tn(score_grad, kv[m, :, cols])
-            dq[m * ROWS : (m + 1) * ROWS, cols] = (gather_heads(stacked) * SCALE).astype(BF16)
-            return carry
-
-        lax.fori_loop(0, GROUPS, group, 0)
-
+            return carry
+
+        lax.fori_loop(0, GROUPS, group, 0, unroll=True)
+
+    def stage_project(m):
         def project(c, carry):
             cols = pl.ds(pl.multiple_of(c * CHUNK, CHUNK), CHUNK)
-            result = dot_nt(part[m], w_in[cols, WIDTH : 3 * WIDTH])
-            ng[m, :, cols] = result[0:ROWS]
+            result = dot_nt(part[m, ROWS:KEYS, :], w_in[cols, WIDTH : 3 * WIDTH])
             for k in reversed(range(LEVELS)):
-                sbuf[m, c, k] = result[(k + 1) * ROWS : (k + 2) * ROWS].astype(BF16)
+                sbuf[m, c, k] = result[k * ROWS : (k + 1) * ROWS].astype(BF16)
 
                 @pl.when(t >= steps[k])
                 def _():
@@ -320,9 +346,21 @@
 
         lax.fori_loop(0, CHUNKS, project, 0)
 
+    def stage_query(m):
+        def group(g, carry):
+            cols = pl.ds(pl.multiple_of(g * GROUP, GROUP), GROUP)
+            stacked = dot_tn(sg[g], kv[m, :, cols])
+            dq[m * ROWS : (m + 1) * ROWS, cols] = (gather_heads(stacked) * SCALE).astype(BF16)
+            return carry
+
+        lax.fori_loop(0, GROUPS, group, 0, unroll=True)
+
+    def stage_own(m):
         def own(c, carry):
             cols = pl.ds(pl.multiple_of(c * CHUNK, CHUNK), CHUNK)
-            ng[m, :, cols] += dot_nt(dq[m * ROWS : (m + 1) * ROWS, :], w_in[cols, 0:WIDTH])
+            ng[m, :, cols] = dot_nt(
+                dq[m * ROWS : (m + 1) * ROWS, :], w_in[cols, 0:WIDTH]
+            ) + dot_nt(part[m, 0:ROWS, :], w_in[cols, WIDTH : 3 * WIDTH])
             return carry
 
         lax.fori_loop(0, CHUNKS, own, 0)
@@ -340,13 +378,17 @@
         grad = ng[m]
         value = normed[m]
         inner = jnp.mean(grad * value, axis=-1, keepdims=True)
-        result = (inc[m].astype(F32) + inv[m, :, 0:1] * (grad - value * inner)).astype(BF16)
-        dacts_ref[m] = result
-        gsend[m] = result
-
-        @pl.when(z > 0)
-        def _():
-            z_copy(m).start()
+        for h in range(2):
+            cols = slice(h * COLS, (h + 1) * COLS)
+            change = inv[m, :, 0:1] * (grad[:, cols] - value[:, cols] * inner)
+            result = (inc[m, :, cols].astype(F32) + change).astype(BF16)
+            gsend[m, :, cols] = result
+
+            @pl.when(z > 0)
+            def _():
+                z_copy(m, h).start()
+
+            dacts_ref[m, :, cols] = result
 
     def remote(src, dst, send_sem, recv_sem, peer):
         return pltpu.make_async_remote_copy(
@@ -400,16 +442,15 @@
 
     def operands(i):
         if i < 2:
-            return own_t, dq[:, i * COLS : (i + 1) * COLS], i * COLS
-        if i < 4:
+            low = i * COLS
+            right = inc[:, :, low : low + COLS].reshape(MB * ROWS, COLS)
+            return att_t, right, 3 * WIDTH + low
+        if i < 6:
             low = (i - 2) * COLS
-            return (
-                att_t,
-                inc[:, :, low : low + COLS].reshape(MB * ROWS, COLS),
-                3 * WIDTH + low,
-            )
-        low = (i - 4) * COLS
-        return n_t, part[:, :, low : low + COLS].reshape(MB * KEYS, COLS), WIDTH + low
+            right = part[:, :, low : low + COLS].reshape(MB * KEYS, COLS)
+            return n_t, right, WIDTH + low
+        low = (i - 6) * COLS
+        return own_t, dq[:, low : low + COLS], low
 
     def weight_part(i):
         left, right, _ = operands(i)
@@ -475,34 +516,75 @@
         for side in range(2):
             ring_copy(3, i, side).wait_recv()
         result = pick_row(i, 0) + recv4[i, 0].astype(F32) + recv4[i, 1].astype(F32)
-        low = operands(i)[2]
+        low = (3 * WIDTH if i < 2 else WIDTH - 2 * COLS if i < 6 else -6 * COLS) + i * COLS
         if low < 3 * WIDTH:
             dwin_ref[:, low : low + COLS] = result
         else:
             dwout_ref[:, low - 3 * WIDTH : low - 3 * WIDTH + COLS] = result
 
+    def rest_forward():
+        attend(0)
+        attend(1)
+        transpose_rows()
+
+    last = z == sections - 1
     forward(0)
-    backward_send(0)
-    forward(1)
-    attend(0)
-    attend(1)
+
+    @pl.when(z < sections - 1)
+    def _():
+        forward(1)
+        rest_forward()
+
+    stage_upstream(0)
+    stage_parts(0)
+    stage_project(0)
+
+    @pl.when(last)
+    def _():
+        forward(1)
+
+    stage_query(0)
+    stage_own(0)
     backward_finish(0)
-    transpose_rows()
-    backward_send(1)
+
+    @pl.when(z == 0)
+    def _():
+        wait_incoming(1, 0)
+        wait_incoming(1, 1)
+        weight_part(0)
+        weight_part(1)
+
+    stage_upstream(1)
+    stage_parts(1)
 
     @pl.when(z > 0)
     def _():
+        stage_project(1)
+
+    stage_query(1)
+
+    @pl.when(z > 0)
+    def _():
+        stage_own(1)
         backward_finish(1)
 
-    for i in range(PARTS + 1):
-        if i < PARTS:
-            weight_part(i)
-        if i >= 1:
-            ring_one(i - 1)
+        @pl.when(last)
+        def _():
+            rest_forward()
+
+        weight_part(0)
+        weight_part(1)
+
+    ring_one(0)
+    for i in range(2, PARTS):
+        weight_part(i)
+        ring_one(i - 1)
+    ring_one(PARTS - 1)
 
     @pl.when(z == 0)
     def _():
-        backward_finish(1)
+        stage_project(1)
+        stage_own(1)
 
     for i in range(PARTS + 3):
         if i < PARTS:
@@ -513,6 +595,11 @@
             ring_four(i - 2)
         if i >= 3:
             ring_last(i - 3)
+        if i == PARTS - 1:
+
+            @pl.when(z == 0)
+            def _():
+                backward_finish(1)
 
     for i in range(PARTS):
         pair_copy(i).wait_send()
@@ -534,7 +621,21 @@
 
         @pl.when(z > 0)
         def _():
-            z_copy(m).wait_send()
+            for h in range(2):
+                z_copy(m, h).wait_send()
+
+
+def result_kernel(a, b, c, a_out, b_out, c_out, a_buf, b_buf, c_buf, sem_in, sem_out):
+    sources, buffers, targets = (a, b, c), (a_buf, b_buf, c_buf), (a_out, b_out, c_out)
+    fetch = [pltpu.make_async_copy(sources[i], buffers[i], sem_in.at[i]) for i in range(3)]
+    store = [pltpu.make_async_copy(buffers[i], targets[i], sem_out.at[i]) for i in range(3)]
+    for copy in fetch:
+        copy.start()
+    for i in range(3):
+        fetch[i].wait()
+        store[i].start()
+    for copy in store:
+        copy.wait()
 
 
 def per_device(acts, grad_top, w_in, w_out, offsets):
@@ -581,8 +682,8 @@
             pltpu.SemaphoreType.DMA((MB, LEVELS)),
             pltpu.SemaphoreType.DMA((MB, CHUNKS, LEVELS)),
             pltpu.SemaphoreType.DMA((MB, CHUNKS, LEVELS)),
-            pltpu.SemaphoreType.DMA((MB,)),
-            pltpu.SemaphoreType.DMA((MB,)),
+            pltpu.SemaphoreType.DMA((MB, 2)),
+            pltpu.SemaphoreType.DMA((MB, 2)),
             pltpu.VMEM((2, SIDE, SIDE, SLICE, MB * KEYS), BF16),
             pltpu.VMEM((2, SIDE, SIDE, SLICE, MB * ROWS), BF16),
             pltpu.VMEM((2, SIDE, SIDE, SLICE, MB * ROWS), BF16),
@@ -601,12 +702,28 @@
             pltpu.SemaphoreType.DMA((PARTS,)),
             pltpu.SemaphoreType.DMA((PARTS,)),
         ]
-        + [pltpu.SemaphoreType.DMA((PARTS, 2))] * 8,
+        + [pltpu.SemaphoreType.DMA((PARTS, 2))] * 8
+        + [
+            pltpu.VMEM((GROUPS, KEYS, GROUP), BF16),
+            pltpu.VMEM((ROWS, WIDTH), F32),
+            pltpu.VMEM((ROWS, WIDTH), BF16),
+        ],
         compiler_params=pltpu.CompilerParams(
             collective_id=0, has_side_effects=True, vmem_limit_bytes=63 * 1024 * 1024
         ),
         name="layer_kernel",
     )(acts[0], grad_top, w_in[0], w_out[0], offsets)
+    results = (d_acts, d_in, d_out)
+    anywhere = pl.BlockSpec(memory_space=pl.ANY)
+    d_acts, d_in, d_out = pl.pallas_call(
+        result_kernel,
+        out_shape=tuple(jax.ShapeDtypeStruct(r.shape, r.dtype) for r in results),
+        in_specs=[anywhere] * 3,
+        out_specs=(anywhere,) * 3,
+        scratch_shapes=[pltpu.VMEM(r.shape, r.dtype) for r in results]
+        + [pltpu.SemaphoreType.DMA((3,)), pltpu.SemaphoreType.DMA((3,))],
+        name="result_kernel",
+    )(*results)
     return (d_acts[None], d_in[None], d_out[None])
 
 

time: 241 us -> 221 us (0.917)
  Pallas kernels: 235 us -> 219 us
  local copies, waits for them, and re-layouts: 5 us -> 0 us
    pallas_call x1, Pallas kernels: 235 us -> 217 us  [per_device(): pl.pallas_call(functools.partial(layer_kernel, sections, shards), out_sha...]
    unnamed x3 -> x0, local copies, waits for them, and re-layouts: 5 us -> none
where the time goes in v3:
time: 221 us; the launch traced here: 220 us
  Pallas kernels  219 us (99%)
    pallas_call x1, Pallas kernels, per_device(): pl.pallas_call(functools.partial(layer_kernel, sections, shards), out_sha...  217 us

profile of v3, /device:TPU:2, one launch (start us, length us, event | category | flops | bytes accessed | tf_op | source)
XLA Modules:
  0.0 219.6 jit_solution(7533646683350800074)
XLA Ops:
  0.6 216.9 %layer_kernel.1 = (bf16[2,64,1024]{2,1,0:T(8,128)(2,1)}, f32[32,3072]{1,0:T(8,128)}, f32[32,1024]{1,0:T(8,128)}) custom-call(bf16[2,64,1024]{2,1,0:T(8,128)(2,1)} %bitcast.8, bf16[2,64,1024]{2,1,0:T(8,128)(2,1)} %gtop_ref.1, bf16[1024,3072]{1,0:T(8,128)(2,1)} %bitcast.6, bf16[1024,1024]{1,0:T(8,128)(2,1)} %bitcast.7, s32[1,5]{1,0:T(1,128)} %off_ref.1), custom_call_target="tpu_custom_call" | custom-call | tf_op jit(solution)/shard_map/layer_kernel/pallas_call | solution.py:645
  217.5 1.9 result_kernel.1

commit v4 on v3

--- a/solution.py
+++ b/solution.py
@@ -25,6 +25,8 @@
 CHUNKS = WIDTH // CHUNK
 PER = GROUP // HEAD_DIM
 SIDE = 4
+ROW = 8
+CROSS = 3
 SLICE = 32
 PARTS = 8
 COLS = 512
@@ -111,6 +113,16 @@
     sg,
     up32,
     up16,
+    qbuf,
+    direct,
+    qs,
+    qr,
+    fq,
+    direct1,
+    pbuf,
+    bp,
+    bq,
+    fp,
 ):
     z = lax.axis_index("section")
     t = lax.axis_index("tm")
@@ -119,6 +131,38 @@
     place_y = lax.rem(t // 2, SIDE)
     core = lax.rem(t, 2)
     partner = t + 1 - 2 * core
+    column_of = lax.rem(t, ROW)
+
+    def sends_direct_down(k):
+        if k == 0:
+            return core == 1
+        ok = t >= steps[k]
+        return ok & (column_of >= steps[k]) if k < CROSS else ok
+
+    def gets_direct_down(k):
+        if k == 0:
+            return core == 0
+        ok = t + steps[k] < shards
+        return ok & (column_of + steps[k] < ROW) if k < CROSS else ok
+
+    def sends_direct_up(k):
+        return gets_direct_down(k)
+
+    def sends_cross(k):
+        return (t >= ROW) & (column_of < steps[k])
+
+    def relays(k):
+        return (t >= ROW) & (column_of + steps[k] >= ROW)
+
+    joins = (core == 1) & (t >= 3)
+    gives = (core == 0) & (t >= 2)
+    relay = (t >= ROW) & (column_of >= ROW // 2)
+
+    def cross_target(k):
+        return lax.rem(t + ROW - steps[k], shards)
+
+    def cross_back(k):
+        return lax.rem(t + shards - ROW + steps[k], shards)
 
     def along(axis, step):
         if axis == 0:
@@ -141,7 +185,9 @@
         pl.semaphore_signal(barrier, inc=1, device_id=(z, up_shard(k)), device_id_type=MESH)
         if 2 * steps[k] != shards:
             pl.semaphore_signal(barrier, inc=1, device_id=(z, down_shard(k)), device_id_type=MESH)
-    for peer in (along(1, 1), along(1, -1), partner):
+    peers = (along(1, 1), along(1, -1), partner)
+    peers += (cross_target(1), cross_back(1))
+    for peer in peers:
         pl.semaphore_signal(barrier, inc=1, device_id=(z, peer), device_id_type=MESH)
     for step in (1, sections - 1):
         pl.semaphore_signal(
@@ -165,6 +211,46 @@
             send_sem=bs.at[m, c, k],
             recv_sem=br.at[m, c, k],
             device_id=(z, down_shard(k)),
+            device_id_type=MESH,
+        )
+
+    def cross_copy(m, c, k):
+        return pltpu.make_async_remote_copy(
+            src_ref=sbuf.at[m, c, k],
+            dst_ref=qbuf.at[m, c, k],
+            send_sem=qs.at[m, c, k],
+            recv_sem=qr.at[m, c, k],
+            device_id=(z, cross_target(k)),
+            device_id_type=MESH,
+        )
+
+    def fwd_cross(m, k):
+        return pltpu.make_async_remote_copy(
+            src_ref=nall.at[m, CROSS + 1],
+            dst_ref=nall.at[m, k + 1],
+            send_sem=fq.at[m, k],
+            recv_sem=fr.at[m, k],
+            device_id=(z, cross_back(k)),
+            device_id_type=MESH,
+        )
+
+    def join_copy(m, c):
+        return pltpu.make_async_remote_copy(
+            src_ref=sbuf.at[m, c, 0],
+            dst_ref=pbuf.at[m, c],
+            send_sem=bp.at[m, c],
+            recv_sem=bq.at[m, c],
+            device_id=(z, partner),
+            device_id_type=MESH,
+        )
+
+    def fwd_pair(m):
+        return pltpu.make_async_remote_copy(
+            src_ref=nall.at[m, 2],
+            dst_ref=nall.at[m, 1],
+            send_sem=fp.at[m],
+            recv_sem=fr.at[m, 0],
+            device_id=(z, partner),
             device_id_type=MESH,
         )
 
@@ -179,6 +265,13 @@
             device_id_type=MESH,
         )
 
+    def forward_send(m, levels):
+        for k in levels:
+
+            @pl.when(sends_direct_up(k))
+            def _():
+                fwd_copy(m, k).start()
+
     for m in range(MB):
         x = acts_ref[m].astype(F32)
         inverse = lax.rsqrt(jnp.mean(x * x, axis=-1, keepdims=True) + EPSILON)
@@ -187,12 +280,11 @@
         inv[m] = jnp.broadcast_to(inverse, (ROWS, 128))
         nall[m, 0] = value.astype(BF16)
         if m == 0:
-            pl.semaphore_wait(barrier, 2 * LEVELS + 4)
-        for k in reversed(range(LEVELS)):
-
-            @pl.when(t + steps[k] < shards)
-            def _():
-                fwd_copy(m, k).start()
+            pl.semaphore_wait(barrier, 2 * LEVELS + 6)
+        if m == 0:
+            forward_send(0, (3, 4, 2, 1, 0))
+        else:
+            forward_send(1, (3,))
 
         for k in range(LEVELS):
 
@@ -235,8 +327,6 @@
             qm[m, c] = spread(result[m * ROWS : (m + 1) * ROWS])
         return carry
 
-    lax.fori_loop(0, GROUPS, own_query, 0)
-
     def own_pair(c, carry):
         cols = pl.ds(pl.multiple_of(c * GROUP, GROUP), GROUP)
         source = pl.ds(pl.multiple_of(WIDTH + c * GROUP, GROUP), GROUP)
@@ -246,10 +336,32 @@
             kv[m, 0:ROWS, cols] = result[m * ROWS : (m + 1) * ROWS]
         return carry
 
-    lax.fori_loop(0, 2 * GROUPS, own_pair, 0)
+    def own_projections():
+        lax.fori_loop(0, GROUPS, own_query, 0, unroll=2)
+        lax.fori_loop(0, 2 * GROUPS, own_pair, 0, unroll=2)
+
+    def forward_relay(m):
+        @pl.when(t >= steps[CROSS])
+        def _():
+            fwd_copy(m, CROSS).wait_recv()
+
+        for k in reversed(range(1, CROSS)):
+
+            @pl.when(relays(k))
+            def _():
+                fwd_cross(m, k).start()
+
+    def forward_join(m):
+        @pl.when(t >= steps[1])
+        def _():
+            fwd_copy(m, 1).wait_recv()
+
+        @pl.when(joins)
+        def _():
+            fwd_pair(m).start()
 
     def forward(m):
-        for k in range(LEVELS):
+        for k in (0, 2, 4):
 
             @pl.when(t >= steps[k])
             def _():
@@ -335,16 +447,75 @@
         def project(c, carry):
             cols = pl.ds(pl.multiple_of(c * CHUNK, CHUNK), CHUNK)
             result = dot_nt(part[m, ROWS:KEYS, :], w_in[cols, WIDTH : 3 * WIDTH])
-            for k in reversed(range(LEVELS)):
-                sbuf[m, c, k] = result[k * ROWS : (k + 1) * ROWS].astype(BF16)
-
-                @pl.when(t >= steps[k])
+            for k in (2, 0, 1, 4, 3):
+                term = result[k * ROWS : (k + 1) * ROWS]
+                sbuf[m, c, k] = term.astype(BF16)
+                send = sends_direct_down(k)
+                if k == 0:
+
+                    @pl.when(gives)
+                    def _():
+                        join_copy(m, c).start()
+
+                if k == 1:
+                    direct1[c] = term
+                    send = send & jnp.logical_not(joins)
+
+                    @pl.when(sends_cross(k) & jnp.logical_not(joins))
+                    def _():
+                        cross_copy(m, c, k).start()
+
+                if k == 2:
+
+                    @pl.when(sends_cross(k))
+                    def _():
+                        cross_copy(m, c, k).start()
+
+                if k == CROSS:
+                    direct[c] = term
+                    send = send & jnp.logical_not(relay)
+
+                @pl.when(send)
                 def _():
                     bwd_copy(m, c, k).start()
 
+            @pl.when(joins & (c > 0))
+            def _():
+                join_send(m, c - 1)
+
             return carry
 
+        def join_send(m, c):
+            join_copy(m, c).wait_recv()
+            sbuf[m, c, 1] = (direct1[c] + pbuf[m, c].astype(F32)).astype(BF16)
+
+            @pl.when(sends_direct_down(1))
+            def _():
+                bwd_copy(m, c, 1).start()
+
+            @pl.when(sends_cross(1))
+            def _():
+                cross_copy(m, c, 1).start()
+
         lax.fori_loop(0, CHUNKS, project, 0)
+
+        @pl.when(joins)
+        def _():
+            join_send(m, CHUNKS - 1)
+
+    def stage_relay(m):
+        @pl.when(relay)
+        def _():
+            for c in range(CHUNKS):
+                for k in reversed(range(1, CROSS)):
+
+                    @pl.when(relays(k))
+                    def _():
+                        cross_copy(m, c, k).wait_recv()
+                        direct[c] += qbuf[m, c, k].astype(F32)
+
+                sbuf[m, c, CROSS] = direct[c].astype(BF16)
+                bwd_copy(m, c, CROSS).start()
 
     def stage_query(m):
         def group(g, carry):
@@ -369,7 +540,7 @@
         for c in range(CHUNKS):
             for k in range(LEVELS):
 
-                @pl.when(t + steps[k] < shards)
+                @pl.when(gets_direct_down(k))
                 def _():
                     bwd_copy(m, c, k).wait_recv()
                     cols = slice(c * CHUNK, (c + 1) * CHUNK)
@@ -528,7 +699,13 @@
         transpose_rows()
 
     last = z == sections - 1
+    forward_relay(0)
+    forward_send(1, (4, 2, 1, 0))
+    own_projections()
+    forward_join(0)
+    forward_relay(1)
     forward(0)
+    forward_join(1)
 
     @pl.when(z < sections - 1)
     def _():
@@ -544,6 +721,7 @@
         forward(1)
 
     stage_query(0)
+    stage_relay(0)
     stage_own(0)
     backward_finish(0)
 
@@ -555,6 +733,12 @@
         weight_part(1)
 
     stage_upstream(1)
+
+    @pl.when(z == 0)
+    def _():
+        ring_one(0)
+        ring_one(1)
+
     stage_parts(1)
 
     @pl.when(z > 0)
@@ -565,6 +749,7 @@
 
     @pl.when(z > 0)
     def _():
+        stage_relay(1)
         stage_own(1)
         backward_finish(1)
 
@@ -574,17 +759,20 @@
 
         weight_part(0)
         weight_part(1)
-
-    ring_one(0)
+        ring_one(0)
+        ring_one(1)
+
     for i in range(2, PARTS):
         weight_part(i)
-        ring_one(i - 1)
+        if i > 2:
+            ring_one(i - 1)
     ring_one(PARTS - 1)
 
     @pl.when(z == 0)
     def _():
         stage_project(1)
         stage_own(1)
+        stage_relay(1)
 
     for i in range(PARTS + 3):
         if i < PARTS:
@@ -610,14 +798,34 @@
     for m in range(MB):
         for k in range(LEVELS):
 
-            @pl.when(t + steps[k] < shards)
+            @pl.when(sends_direct_up(k))
             def _():
                 fwd_copy(m, k).wait_send()
 
-            @pl.when(t >= steps[k])
+            @pl.when(sends_direct_down(k))
             def _():
                 for c in range(CHUNKS):
                     bwd_copy(m, c, k).wait_send()
+
+            if 0 < k < CROSS:
+
+                @pl.when(relays(k))
+                def _():
+                    fwd_cross(m, k).wait_send()
+
+                @pl.when(sends_cross(k))
+                def _():
+                    for c in range(CHUNKS):
+                        cross_copy(m, c, k).wait_send()
+
+        @pl.when(joins)
+        def _():
+            fwd_pair(m).wait_send()
+
+        @pl.when(gives)
+        def _():
+            for c in range(CHUNKS):
+                join_copy(m, c).wait_send()
 
         @pl.when(z > 0)
         def _():
@@ -707,6 +915,16 @@
             pltpu.VMEM((GROUPS, KEYS, GROUP), BF16),
             pltpu.VMEM((ROWS, WIDTH), F32),
             pltpu.VMEM((ROWS, WIDTH), BF16),
+            pltpu.VMEM((MB, CHUNKS, CROSS, ROWS, CHUNK), BF16),
+            pltpu.VMEM((CHUNKS, ROWS, CHUNK), F32),
+            pltpu.SemaphoreType.DMA((MB, CHUNKS, CROSS)),
+            pltpu.SemaphoreType.DMA((MB, CHUNKS, CROSS)),
+            pltpu.SemaphoreType.DMA((MB, CROSS)),
+            pltpu.VMEM((CHUNKS, ROWS, CHUNK), F32),
+            pltpu.VMEM((MB, CHUNKS, ROWS, CHUNK), BF16),
+            pltpu.SemaphoreType.DMA((MB, CHUNKS)),
+            pltpu.SemaphoreType.DMA((MB, CHUNKS)),
+            pltpu.SemaphoreType.DMA((MB,)),
         ],
         compiler_params=pltpu.CompilerParams(
             collective_id=0, has_side_effects=True, vmem_limit_bytes=63 * 1024 * 1024

time: 221 us -> 209 us (0.946)
  Pallas kernels: 219 us -> 208 us
    pallas_call x1, Pallas kernels: 217 us -> 206 us  [per_device(): pl.pallas_call(functools.partial(layer_kernel, sections, shards), out_sha...]
where the time goes in v4:
time: 209 us
  Pallas kernels  208 us (100%)
    pallas_call x1, Pallas kernels, per_device(): pl.pallas_call(functools.partial(layer_kernel, sections, shards), out_sha...  206 us

profile of v4, /device:TPU:2, one launch (start us, length us, event | category | flops | bytes accessed | tf_op | source)
XLA Modules:
  0.0 209.1 jit_solution(1514818898484685625)
XLA Ops:
  0.6 206.4 %layer_kernel.1 = (bf16[2,64,1024]{2,1,0:T(8,128)(2,1)}, f32[32,3072]{1,0:T(8,128)}, f32[32,1024]{1,0:T(8,128)}) custom-call(bf16[2,64,1024]{2,1,0:T(8,128)(2,1)} %bitcast.8, bf16[2,64,1024]{2,1,0:T(8,128)(2,1)} %gtop_ref.1, bf16[1024,3072]{1,0:T(8,128)(2,1)} %bitcast.6, bf16[1024,1024]{1,0:T(8,128)(2,1)} %bitcast.7, s32[1,5]{1,0:T(1,128)} %off_ref.1), custom_call_target="tpu_custom_call" | custom-call | tf_op jit(solution)/shard_map/layer_kernel/pallas_call | solution.py:853
  207.0 1.9 result_kernel.1

commit v5 on v4

--- a/solution.py
+++ b/solution.py
@@ -316,9 +316,6 @@
             total = jnp.where(lanes == head, stacked[head * ROWS : (head + 1) * ROWS], total)
         return total
 
-    copy_in.wait()
-    copy_out.wait()
-
     def own_query(c, carry):
         cols = pl.ds(pl.multiple_of(c * GROUP, GROUP), GROUP)
         both = jnp.concatenate([nall[0, 0], nall[1, 0]], 0)
@@ -360,7 +357,7 @@
         def _():
             fwd_pair(m).start()
 
-    def forward(m):
+    def forward_keys(m):
         for k in (0, 2, 4):
 
             @pl.when(t >= steps[k])
@@ -376,6 +373,7 @@
 
         lax.fori_loop(0, 2 * GROUPS, far_pair, 0, unroll=2)
 
+    def forward_weights(m):
         def probability(g, carry):
             cols = pl.ds(pl.multiple_of(g * GROUP, GROUP), GROUP)
             scores = dot_nt(kv[m, :, cols], qm[m, g]) * SCALE + bias[...]
@@ -616,12 +614,12 @@
             low = i * COLS
             right = inc[:, :, low : low + COLS].reshape(MB * ROWS, COLS)
             return att_t, right, 3 * WIDTH + low
-        if i < 6:
+        if i < 4:
             low = (i - 2) * COLS
-            right = part[:, :, low : low + COLS].reshape(MB * KEYS, COLS)
-            return n_t, right, WIDTH + low
-        low = (i - 6) * COLS
-        return own_t, dq[:, low : low + COLS], low
+            return own_t, dq[:, low : low + COLS], low
+        low = (i - 4) * COLS
+        right = part[:, :, low : low + COLS].reshape(MB * KEYS, COLS)
+        return n_t, right, WIDTH + low
 
     def weight_part(i):
         left, right, _ = operands(i)
@@ -687,7 +685,7 @@
         for side in range(2):
             ring_copy(3, i, side).wait_recv()
         result = pick_row(i, 0) + recv4[i, 0].astype(F32) + recv4[i, 1].astype(F32)
-        low = (3 * WIDTH if i < 2 else WIDTH - 2 * COLS if i < 6 else -6 * COLS) + i * COLS
+        low = (3 * WIDTH if i < 2 else -2 * COLS if i < 4 else WIDTH - 4 * COLS) + i * COLS
         if low < 3 * WIDTH:
             dwin_ref[:, low : low + COLS] = result
         else:
@@ -701,15 +699,19 @@
     last = z == sections - 1
     forward_relay(0)
     forward_send(1, (4, 2, 1, 0))
+    copy_in.wait()
     own_projections()
     forward_join(0)
     forward_relay(1)
-    forward(0)
+    forward_keys(0)
+    forward_weights(0)
     forward_join(1)
+    copy_out.wait()
 
     @pl.when(z < sections - 1)
     def _():
-        forward(1)
+        forward_keys(1)
+        forward_weights(1)
         rest_forward()
 
     stage_upstream(0)
@@ -718,10 +720,15 @@
 
     @pl.when(last)
     def _():
-        forward(1)
+        forward_keys(1)
 
     stage_query(0)
     stage_relay(0)
+
+    @pl.when(last)
+    def _():
+        forward_weights(1)
+
     stage_own(0)
     backward_finish(0)
 
@@ -766,28 +773,38 @@
         weight_part(i)
         if i > 2:
             ring_one(i - 1)
+            ring_two(i - 3)
     ring_one(PARTS - 1)
+    ring_two(PARTS - 3)
 
     @pl.when(z == 0)
     def _():
         stage_project(1)
         stage_own(1)
+
+    ring_three(0)
+    ring_two(PARTS - 2)
+    ring_three(1)
+    ring_two(PARTS - 1)
+
+    @pl.when(z == 0)
+    def _():
         stage_relay(1)
 
-    for i in range(PARTS + 3):
+    for i in range(2, PARTS + 3):
         if i < PARTS:
-            ring_two(i)
-        if 1 <= i <= PARTS:
-            ring_three(i - 1)
-        if 2 <= i <= PARTS + 1:
+            ring_three(i)
+        if i < PARTS + 2:
             ring_four(i - 2)
-        if i >= 3:
-            ring_last(i - 3)
+        if 4 <= i:
+            ring_last(i - 4)
         if i == PARTS - 1:
 
             @pl.when(z == 0)
             def _():
                 backward_finish(1)
+
+    ring_last(PARTS - 1)
 
     for i in range(PARTS):
         pair_copy(i).wait_send()

time: 209 us -> 200 us (0.957)
  Pallas kernels: 208 us -> 198 us
    pallas_call x1, Pallas kernels: 206 us -> 196 us  [per_device(): pl.pallas_call(functools.partial(layer_kernel, sections, shards), out_sha...]
where the time goes in v5:
time: 200 us; the launch traced here: 199 us
  Pallas kernels  198 us (99%)
    pallas_call x1, Pallas kernels, per_device(): pl.pallas_call(functools.partial(layer_kernel, sections, shards), out_sha...  196 us

profile of v5, /device:TPU:2, one launch (start us, length us, event | category | flops | bytes accessed | tf_op | source)
XLA Modules:
  0.0 199.0 jit_solution(1452118284846538682)
XLA Ops:
  0.6 196.2 %layer_kernel.1 = (bf16[2,64,1024]{2,1,0:T(8,128)(2,1)}, f32[32,3072]{1,0:T(8,128)}, f32[32,1024]{1,0:T(8,128)}) custom-call(bf16[2,64,1024]{2,1,0:T(8,128)(2,1)} %bitcast.8, bf16[2,64,1024]{2,1,0:T(8,128)(2,1)} %gtop_ref.1, bf16[1024,3072]{1,0:T(8,128)(2,1)} %bitcast.6, bf16[1024,1024]{1,0:T(8,128)(2,1)} %bitcast.7, s32[1,5]{1,0:T(1,128)} %off_ref.1), custom_call_target="tpu_custom_call" | custom-call | tf_op jit(solution)/shard_map/layer_kernel/pallas_call | solution.py:870
  196.9 1.9 result_kernel.1

commit v6 on v5

--- a/solution.py
+++ b/solution.py
@@ -306,6 +306,12 @@
     def _():
         inc[...] = gtop_ref[...]
 
+    for k in range(LEVELS):
+
+        @pl.when(jnp.logical_not(gets_direct_down(k)))
+        def _():
+            rbuf[:, :, k] = jnp.zeros((MB, CHUNKS, ROWS, CHUNK), BF16)
+
     def spread(rows):
         return jnp.concatenate([rows] * PER, 0) * bm[...]
 
@@ -442,10 +448,11 @@
         lax.fori_loop(0, GROUPS, group, 0, unroll=True)
 
     def stage_project(m):
-        def project(c, carry):
+        def near(c, carry):
             cols = pl.ds(pl.multiple_of(c * CHUNK, CHUNK), CHUNK)
-            result = dot_nt(part[m, ROWS:KEYS, :], w_in[cols, WIDTH : 3 * WIDTH])
-            for k in (2, 0, 1, 4, 3):
+            rows = part[m, ROWS : (CROSS + 1) * ROWS, :]
+            result = dot_nt(rows, w_in[cols, WIDTH : 3 * WIDTH])
+            for k in (2, 0, 1):
                 term = result[k * ROWS : (k + 1) * ROWS]
                 sbuf[m, c, k] = term.astype(BF16)
                 send = sends_direct_down(k)
@@ -469,6 +476,42 @@
                     def _():
                         cross_copy(m, c, k).start()
 
+                @pl.when(send)
+                def _():
+                    bwd_copy(m, c, k).start()
+
+            return carry
+
+        def join_send(c):
+            join_copy(m, c).wait_recv()
+            sbuf[m, c, 1] = (direct1[c] + pbuf[m, c].astype(F32)).astype(BF16)
+
+            @pl.when(sends_direct_down(1))
+            def _():
+                bwd_copy(m, c, 1).start()
+
+            @pl.when(sends_cross(1))
+            def _():
+                cross_copy(m, c, 1).start()
+
+        def far(c, carry):
+            @pl.when(joins & (c == 0))
+            def _():
+                join_send(0)
+                join_send(1)
+
+            @pl.when(joins & (c == 2))
+            def _():
+                join_send(2)
+
+            cols = pl.ds(pl.multiple_of(c * CHUNK, CHUNK), CHUNK)
+            rows = jnp.concatenate([part[m, 0:ROWS, :], part[m, (CROSS + 1) * ROWS : KEYS, :]], 0)
+            result = dot_nt(rows, w_in[cols, WIDTH : 3 * WIDTH])
+            ng[m, :, cols] = result[0:ROWS]
+            for k in (4, 3):
+                term = result[(k - 2) * ROWS : (k - 1) * ROWS]
+                sbuf[m, c, k] = term.astype(BF16)
+                send = sends_direct_down(k)
                 if k == CROSS:
                     direct[c] = term
                     send = send & jnp.logical_not(relay)
@@ -477,29 +520,14 @@
                 def _():
                     bwd_copy(m, c, k).start()
 
-            @pl.when(joins & (c > 0))
-            def _():
-                join_send(m, c - 1)
-
             return carry
 
-        def join_send(m, c):
-            join_copy(m, c).wait_recv()
-            sbuf[m, c, 1] = (direct1[c] + pbuf[m, c].astype(F32)).astype(BF16)
-
-            @pl.when(sends_direct_down(1))
-            def _():
-                bwd_copy(m, c, 1).start()
-
-            @pl.when(sends_cross(1))
-            def _():
-                cross_copy(m, c, 1).start()
-
-        lax.fori_loop(0, CHUNKS, project, 0)
+        lax.fori_loop(0, CHUNKS, near, 0)
+        lax.fori_loop(0, CHUNKS, far, 0)
 
         @pl.when(joins)
         def _():
-            join_send(m, CHUNKS - 1)
+            join_send(3)
 
     def stage_relay(m):
         @pl.when(relay)
@@ -527,24 +555,34 @@
     def stage_own(m):
         def own(c, carry):
             cols = pl.ds(pl.multiple_of(c * CHUNK, CHUNK), CHUNK)
-            ng[m, :, cols] = dot_nt(
-                dq[m * ROWS : (m + 1) * ROWS, :], w_in[cols, 0:WIDTH]
-            ) + dot_nt(part[m, 0:ROWS, :], w_in[cols, WIDTH : 3 * WIDTH])
+            ng[m, :, cols] += dot_nt(dq[m * ROWS : (m + 1) * ROWS, :], w_in[cols, 0:WIDTH])
             return carry
 
         lax.fori_loop(0, CHUNKS, own, 0)
 
     def backward_finish(m):
+        early = (0, 1, 2, 4)
         for c in range(CHUNKS):
-            for k in range(LEVELS):
+            cols = slice(c * CHUNK, (c + 1) * CHUNK)
+            for k in early:
 
                 @pl.when(gets_direct_down(k))
                 def _():
                     bwd_copy(m, c, k).wait_recv()
-                    cols = slice(c * CHUNK, (c + 1) * CHUNK)
-                    ng[m, :, cols] += rbuf[m, c, k].astype(F32)
-
-        grad = ng[m]
+
+            ng[m, :, cols] += sum(rbuf[m, c, k].astype(F32) for k in early)
+
+        for c in range(CHUNKS):
+
+            @pl.when(gets_direct_down(CROSS))
+            def _():
+                bwd_copy(m, c, CROSS).wait_recv()
+
+        pieces = []
+        for c in range(CHUNKS):
+            cols = slice(c * CHUNK, (c + 1) * CHUNK)
+            pieces.append(ng[m, :, cols] + rbuf[m, c, CROSS].astype(F32))
+        grad = jnp.concatenate(pieces, 1)
         value = normed[m]
         inner = jnp.mean(grad * value, axis=-1, keepdims=True)
         for h in range(2):

time: 200 us -> 197 us (0.985)
  Pallas kernels: 198 us -> 195 us
    pallas_call x1, Pallas kernels: 196 us -> 193 us  [per_device(): pl.pallas_call(functools.partial(layer_kernel, sections, shards), out_sha...]
where the time goes in v6:
time: 197 us; the launch traced here: 196 us
  Pallas kernels  195 us (99%)
    pallas_call x1, Pallas kernels, per_device(): pl.pallas_call(functools.partial(layer_kernel, sections, shards), out_sha...  193 us

profile of v6, /device:TPU:2, one launch (start us, length us, event | category | flops | bytes accessed | tf_op | source)
XLA Modules:
  0.0 196.1 jit_solution(2878079866276185067)
XLA Ops:
  0.6 193.3 %layer_kernel.1 = (bf16[2,64,1024]{2,1,0:T(8,128)(2,1)}, f32[32,3072]{1,0:T(8,128)}, f32[32,1024]{1,0:T(8,128)}) custom-call(bf16[2,64,1024]{2,1,0:T(8,128)(2,1)} %bitcast.8, bf16[2,64,1024]{2,1,0:T(8,128)(2,1)} %gtop_ref.1, bf16[1024,3072]{1,0:T(8,128)(2,1)} %bitcast.6, bf16[1024,1024]{1,0:T(8,128)(2,1)} %bitcast.7, s32[1,5]{1,0:T(1,128)} %off_ref.1), custom_call_target="tpu_custom_call" | custom-call | tf_op jit(solution)/shard_map/layer_kernel/pallas_call | solution.py:908
  194.0 1.9 result_kernel.1

commit v7 on v6

--- a/solution.py
+++ b/solution.py
@@ -779,12 +779,12 @@
 
     stage_upstream(1)
 
+    stage_parts(1)
+
     @pl.when(z == 0)
     def _():
         ring_one(0)
         ring_one(1)
-
-    stage_parts(1)
 
     @pl.when(z > 0)
     def _():

time: 197 us -> 196 us (level)
  no operation moved by 1% of the time
where the time goes in v7:
time: 196 us; the launch traced here: 195 us
  Pallas kernels  195 us (99%)
    pallas_call x1, Pallas kernels, per_device(): pl.pallas_call(functools.partial(layer_kernel, sections, shards), out_sha...  193 us

profile of v7, /device:TPU:2, one launch (start us, length us, event | category | flops | bytes accessed | tf_op | source)
XLA Modules:
  0.0 195.4 jit_solution(14325443825496465496)
XLA Ops:
  0.6 192.7 %layer_kernel.1 = (bf16[2,64,1024]{2,1,0:T(8,128)(2,1)}, f32[32,3072]{1,0:T(8,128)}, f32[32,1024]{1,0:T(8,128)}) custom-call(bf16[2,64,1024]{2,1,0:T(8,128)(2,1)} %bitcast.8, bf16[2,64,1024]{2,1,0:T(8,128)(2,1)} %gtop_ref.1, bf16[1024,3072]{1,0:T(8,128)(2,1)} %bitcast.6, bf16[1024,1024]{1,0:T(8,128)(2,1)} %bitcast.7, s32[1,5]{1,0:T(1,128)} %off_ref.1), custom_call_target="tpu_custom_call" | custom-call | tf_op jit(solution)/shard_map/layer_kernel/pallas_call | solution.py:908
  193.3 1.9 result_kernel.1
